TPU v7x, 512 devices: a whole 4x4x16 slice. The times are simulated.
512 devices in a mesh: seq: 128 (over x, z_lo, y, core), head: 4 (over z_hi).
Axes of the slice: x: 4, y: 4, z: 16 (z_hi: 4, z_lo: 4; z = z_hi * 4 + z_lo), core: 2. Of those that a mesh axis runs over, the one named last changes fastest.
Arguments:
- query_rows: bfloat16 [65536, 2048], P('seq', 'head'), may hold values from -18 to 18
- key_rows: bfloat16 [65536, 2048], P('seq', 'head'), may hold values from -18 to 18
- value_rows: bfloat16 [65536, 2048], P('seq', 'head'), may hold values from -6 to 6
- out_grad: bfloat16 [65536, 4096], P('seq', 'head'), may hold values from -6 to 6
- out_weight: bfloat16 [2048, 4096], P('head', 'seq'), may hold values from -0.09375 to 0.09375
Outputs:
- attended: bfloat16 [65536, 2048], P('seq', 'head')
- query_grad: bfloat16 [65536, 2048], P('seq', 'head')
- key_grad: bfloat16 [65536, 2048], P('seq', 'head')
- value_grad: bfloat16 [65536, 2048], P('seq', 'head')
All inputs are finite; a program needn't handle non-finite values.
Results may differ from a plain program's by a relative error of at most 0.0067.
Values may be sent and summed in bfloat16 or wider, within the bound.
No kernel may reach another device: no remote copies, remote signals or barrier semaphores. Data moves between devices by JAX's collectives and lax.ppermute only.
A program may use at most 64 MiB of HBM per device.

v0:
```python
import jax
import jax.numpy as jnp
from jax import lax
from jax.experimental import pallas as pl
from jax.experimental.pallas import tpu as pltpu
from jax.sharding import Mesh
from jax.sharding import PartitionSpec as P

DH = 128
SCALING = DH ** (-0.5)
SENTINEL = -1e30
SEQ = ("x", "zl", "y", "core")
UNITS = 16
F32 = jnp.float32
BF16 = jnp.bfloat16


def nt(a, b):
    return lax.dot_general(a, b, (((1,), (1,)), ((), ())), preferred_element_type=F32)


def tn(a, b):
    return lax.dot_general(a, b, (((0,), (0,)), ((), ())), preferred_element_type=F32)


def nn(a, b):
    return lax.dot_general(a, b, (((1,), (0,)), ((), ())), preferred_element_type=F32)


def swap_matrix():
    rows = lax.broadcasted_iota(jnp.int32, (256, 256), 0)
    cols = lax.broadcasted_iota(jnp.int32, (256, 256), 1)
    return jnp.where(cols == (rows % 16) * 16 + rows // 16, 1.0, 0.0).astype(BF16)


def one_hot_rows(rows_n, cols_n, row, spread):
    rows = lax.broadcasted_iota(jnp.int32, (rows_n, cols_n), 0)
    cols = lax.broadcasted_iota(jnp.int32, (rows_n, cols_n), 1)
    hit = rows == cols * 8 + row if spread else cols == rows * 8 + row
    return jnp.where(hit, 1.0, 0.0).astype(BF16)


def split_rows(rows):
    hi = rows.astype(BF16).astype(F32)
    mid = (rows - hi).astype(BF16).astype(F32)
    low = (rows - hi - mid).astype(BF16).astype(F32)
    return jnp.concatenate([hi, mid, low, jnp.zeros_like(hi)], axis=0)


def join_rows(parts):
    return parts[0:32] + parts[32:64] + parts[64:96]


def stat_columns(stats):
    return jnp.transpose(split_rows(stats)).astype(BF16)


def take_stats(in_ref, base, row):
    collect = one_hot_rows(16, 128, row, False)
    pieces = []
    for block in range(8):
        rows = in_ref[block * 16 : block * 16 + 16, base : base + 8, :].reshape(128, 128)
        pieces.append(nn(collect, rows))
    return join_rows(jnp.transpose(jnp.concatenate(pieces, axis=0)))


def pack_rows(sources, out_ref):
    swap = swap_matrix()

    def step(block, carry):
        at = pl.multiple_of(block * 16, 16)
        for which, source in enumerate(sources):
            pieces = []
            for unit in range(UNITS):
                row, head = unit // 4, unit % 4
                pieces.append(
                    source[pl.ds(row * 128 + at, 16), head * 128 : head * 128 + 128]
                )
            moved = nn(swap, jnp.concatenate(pieces, axis=0)).astype(BF16)
            out_ref[pl.ds(at, 16), which * 16 : which * 16 + 16, :] = moved.reshape(
                16, 16, 128
            )
        return carry

    lax.fori_loop(0, 8, step, 0)


def pack_kernel(q_ref, k_ref, v_ref, out_ref):
    pack_rows((q_ref, k_ref, v_ref), out_ref)


def masks(strict):
    keys = lax.broadcasted_iota(jnp.int32, (128, 128), 0)
    queries = lax.broadcasted_iota(jnp.int32, (128, 128), 1)
    return keys < queries if strict else keys <= queries


def forward_rows(q, k, visible):
    scores = nt(k, q) * SCALING
    top = jnp.max(jnp.where(visible, scores, SENTINEL), axis=0, keepdims=True)
    weights = jnp.where(visible, jnp.exp(scores - top), 0.0)
    total = jnp.sum(weights, axis=0, keepdims=True)
    return scores, top, weights, total


def far_forward_kernel(
    qkv_ref, unit_ref, probs_ref, out_ref, columns_ref, lse_ref, out_scr
):
    swap = swap_matrix()
    visible = masks(True)

    def unpack(block, carry):
        at = pl.multiple_of(block * 16, 16)
        for which in range(3):
            rows = qkv_ref[pl.ds(at, 16), which * 16 : which * 16 + 16, :].reshape(256, 128)
            unit_ref[which, :, pl.ds(at, 16), :] = (
                nn(swap, rows).astype(BF16).reshape(16, 16, 128)
            )
        return carry

    lax.fori_loop(0, 8, unpack, 0)
    lse_ref[...] = jnp.zeros((32, 128), F32)
    for unit in range(UNITS):
        q, k, v = unit_ref[0, unit], unit_ref[1, unit], unit_ref[2, unit]
        _, top, weights, total = forward_rows(q, k, visible)
        some = total > 0.0
        inverse = jnp.where(some, 1.0 / jnp.where(some, total, 1.0), 0.0)
        probs = weights * inverse
        probs_ref[unit] = probs
        out_scr[unit] = tn(probs.astype(BF16), v).astype(BF16)
        lse_ref[unit : unit + 1, :] = jnp.where(
            some, top + jnp.log(jnp.where(some, total, 1.0)), SENTINEL
        )

    def pack(block, carry):
        at = pl.multiple_of(block * 16, 16)
        rows = out_scr[:, pl.ds(at, 16), :].reshape(256, 128)
        out_ref[pl.ds(at, 16), :, :] = nn(swap, rows).astype(BF16).reshape(16, 16, 128)
        return carry

    lax.fori_loop(0, 8, pack, 0)
    columns_ref[...] = stat_columns(lse_ref[...])


def band_kernel(q_ref, k_ref, v_ref, g_ref, far_ref, columns_ref, out_ref, stats_ref):
    pack_rows((g_ref,), out_ref)
    out_ref[:, 16:32, :] = far_ref[...]
    visible = masks(False)

    for unit in range(UNITS):
        rows = slice((unit // 4) * 128, (unit // 4) * 128 + 128)
        cols = slice((unit % 4) * 128, (unit % 4) * 128 + 128)
        q, k, v, g = q_ref[rows, cols], k_ref[rows, cols], v_ref[rows, cols], g_ref[rows, cols]
        _, top, weights, total = forward_rows(q, k, visible)
        dot = jnp.sum(weights * nt(v, g), axis=0, keepdims=True)
        stats_ref[unit : unit + 1, :] = top + jnp.log(total)
        stats_ref[16 + unit : 17 + unit, :] = dot / total
    columns = stat_columns(stats_ref[...])
    home, away = one_hot_rows(128, 16, 0, True), one_hot_rows(128, 16, 1, True)
    for block in range(8):
        at = slice(block * 16, block * 16 + 16)
        rows = nn(home, columns[at]) + nn(away, columns_ref[at, :])
        out_ref[at, 32:40, :] = rows.astype(BF16).reshape(16, 8, 128)


def combine(band_lse, far_lse):
    highest = jnp.maximum(band_lse, far_lse)
    band_part = jnp.exp(band_lse - highest)
    far_part = jnp.exp(far_lse - highest)
    norm = band_part + far_part
    return highest + jnp.log(norm), band_part / norm, far_part / norm


def far_backward_kernel(unit_ref, probs_ref, lse_ref, g_ref, out_ref, g_scr, out_scr):
    swap = swap_matrix()

    def unpack(block, carry):
        at = pl.multiple_of(block * 16, 16)
        rows = g_ref[pl.ds(at, 16), 0:16, :].reshape(256, 128)
        g_scr[:, pl.ds(at, 16), :] = nn(swap, rows).astype(BF16).reshape(16, 16, 128)
        return carry

    lax.fori_loop(0, 8, unpack, 0)
    band = take_stats(g_ref, 32, 0)
    _, band_share, far_share = combine(band[0:16], lse_ref[0:16, :])
    band_delta = band_share * band[16:32]
    for unit in range(UNITS):
        q, k, v, g = unit_ref[0, unit], unit_ref[1, unit], unit_ref[2, unit], g_scr[unit]
        probs = probs_ref[unit] * far_share[unit : unit + 1]
        dprob = nt(v, g)
        delta = band_delta[unit : unit + 1] + jnp.sum(probs * dprob, axis=0, keepdims=True)
        dscore = (probs * (dprob - delta)).astype(BF16)
        out_scr[0, unit] = (tn(dscore, k) * SCALING).astype(BF16)
        out_scr[1, unit] = (nn(dscore, q) * SCALING).astype(BF16)
        out_scr[2, unit] = nn(probs.astype(BF16), g).astype(BF16)

    def pack(block, carry):
        at = pl.multiple_of(block * 16, 16)
        for which in range(3):
            rows = out_scr[which, :, pl.ds(at, 16), :].reshape(256, 128)
            out_ref[pl.ds(at, 16), which * 16 : which * 16 + 16, :] = (
                nn(swap, rows).astype(BF16).reshape(16, 16, 128)
            )
        return carry

    lax.fori_loop(0, 8, pack, 0)


def band_backward_kernel(
    q_ref, k_ref, v_ref, g_ref, band_ref, far_ref, att_ref, dq_ref, dk_ref, dv_ref, far_scr
):
    swap = swap_matrix()
    visible = masks(False)

    def unpack(block, carry):
        at = pl.multiple_of(block * 16, 16)
        rows = far_ref[pl.ds(at, 16), 16:32, :].reshape(256, 128)
        far_scr[:, pl.ds(at, 16), :] = nn(swap, rows).astype(BF16).reshape(16, 16, 128)
        return carry

    lax.fori_loop(0, 8, unpack, 0)
    far_lse = take_stats(far_ref, 32, 1)[0:16]
    lse, band_share, far_share = combine(band_ref[0:16, :], far_lse)
    band_delta = band_share * band_ref[16:32, :]
    shares = jnp.transpose(
        jnp.concatenate([far_share, jnp.zeros((112, 128), F32)], axis=0)
    )
    ones = jnp.ones((8, 128), BF16)
    for unit in range(UNITS):
        rows = slice((unit // 4) * 128, (unit // 4) * 128 + 128)
        cols = slice((unit % 4) * 128, (unit % 4) * 128 + 128)
        q, k, v, g = q_ref[rows, cols], k_ref[rows, cols], v_ref[rows, cols], g_ref[rows, cols]
        out_far = far_scr[unit].astype(F32)
        product = g.astype(F32) * out_far
        high = product.astype(BF16)
        low = (product - high.astype(F32)).astype(BF16)
        dot_far = (nt(ones, high) + nt(ones, low))[0:1]
        delta = band_delta[unit : unit + 1] + far_share[unit : unit + 1] * dot_far
        scores = nt(k, q) * SCALING
        probs = jnp.where(visible, jnp.exp(scores - lse[unit : unit + 1]), 0.0)
        rounded = probs.astype(BF16)
        dscore = (probs * (nt(v, g) - delta)).astype(BF16)
        att_ref[rows, cols] = (tn(rounded, v) + shares[:, unit : unit + 1] * out_far).astype(BF16)
        dq_ref[rows, cols] = tn(dscore, k) * SCALING
        dk_ref[rows, cols] = nn(dscore, q) * SCALING
        dv_ref[rows, cols] = nn(rounded, g)


def final_kernel(dq_ref, dk_ref, dv_ref, far_ref, query_ref, key_ref, value_ref):
    bands, outs = (dq_ref, dk_ref, dv_ref), (query_ref, key_ref, value_ref)
    rows = lax.broadcasted_iota(jnp.int32, (64, 256), 0)
    cols = lax.broadcasted_iota(jnp.int32, (64, 256), 1)
    source = (rows % 16) * 16 + pl.program_id(0) * 4 + rows // 16
    choose = jnp.where(cols == source, 1.0, 0.0).astype(BF16)
    for block in range(8):
        place = slice(block * 16, block * 16 + 16)
        for which in range(3):
            far = far_ref[place, which * 16 : which * 16 + 16, :].reshape(256, 128)
            moved = nn(choose, far)
            for head in range(4):
                at = slice(head * 128, head * 128 + 128)
                piece = moved[head * 16 : head * 16 + 16]
                outs[which][place, at] = (bands[which][place, at] + piece).astype(BF16)


def final_call(bands, home, shape):
    rows = pl.BlockSpec((128, shape.shape[1]), lambda step: (step, 0))
    whole = pl.BlockSpec(home.shape, lambda step: (0, 0, 0))
    return pl.pallas_call(
        final_kernel,
        grid=(4,),
        out_shape=(shape,) * 3,
        in_specs=[rows] * 3 + [whole],
        out_specs=(rows,) * 3,
        compiler_params=pltpu.CompilerParams(vmem_limit_bytes=16 * 1024 * 1024),
    )(*[pltpu.with_memory_space_constraint(band, pltpu.HBM) for band in bands], home)


def call(kernel, args, outs, scratch=()):
    vmem = pl.BlockSpec(memory_space=pltpu.VMEM)
    single = not isinstance(outs, tuple)
    return pl.pallas_call(
        kernel,
        out_shape=outs,
        in_specs=[vmem] * len(args),
        out_specs=vmem if single else tuple([vmem] * len(outs)),
        scratch_shapes=list(scratch),
        compiler_params=pltpu.CompilerParams(vmem_limit_bytes=24 * 1024 * 1024),
    )(*args)


def shifted(values, axis, by):
    return lax.ppermute(values, axis, [(i, (i + by) % 4) for i in range(4)])


def around(values, axis):
    return jnp.concatenate(
        [values] + [shifted(values, axis, by) for by in (1, 2, 3)], axis=0
    )


def column_order(width):
    zl, y, core = lax.axis_index("zl"), lax.axis_index("y"), lax.axis_index("core")
    rows = lax.broadcasted_iota(jnp.int32, (width, width), 0)
    cols = lax.broadcasted_iota(jnp.int32, (width, width), 1)
    core_at = (cols // 512 + core) % 2
    y_at = (y - (cols // 128) % 4 + 4) % 4
    zl_at = (zl - (cols // 32) % 4 + 4) % 4
    source = zl_at * 256 + y_at * 64 + core_at * 32 + cols % 32
    return (rows == source).astype(BF16)


def program(query_rows, key_rows, value_rows, out_grad, out_weight):
    tokens, width = query_rows.shape
    x, head = lax.axis_index("x"), lax.axis_index("head")

    sent = call(
        pack_kernel,
        (query_rows, key_rows, value_rows),
        jax.ShapeDtypeStruct((128, 48, 128), BF16),
    )
    own = out_weight.T
    weight = lax.ppermute(
        own,
        ("x", "head"),
        [(a * 4 + h, h * 4 + a) for a in range(4) for h in range(4)],
    )
    weight = around(around(weight, "zl"), "y")
    sent, weight = lax.optimization_barrier((sent, weight))
    far_qkv = lax.all_to_all(sent, SEQ, 0, 0, tiled=True)
    mine = jnp.stack([weight] + [shifted(weight, "x", by) for by in (1, 2, 3)])
    others = lax.ppermute(mine, "core", [(0, 1), (1, 0)])
    ordered = jnp.dot(out_grad, column_order(out_grad.shape[1]), preferred_element_type=F32)
    ordered = ordered.astype(BF16)
    far_qkv, others = lax.optimization_barrier((far_qkv, others))

    def partial(target, mine, others):
        at = (x - target + 8) % 4
        near = lax.dynamic_index_in_dim(mine, at, 0, keepdims=False)
        other = lax.dynamic_index_in_dim(others, at, 0, keepdims=False)
        return jnp.dot(ordered[:, :512], near, preferred_element_type=F32) + jnp.dot(
            ordered[:, 512:], other, preferred_element_type=F32
        )

    middle = tokens // 2
    low, high = slice(0, middle), slice(middle, tokens)

    opposite = partial(head + 2, mine, others).astype(BF16)
    opposite, mine, others = lax.optimization_barrier((opposite, mine, others))
    above, below, here = (partial(head + by, mine, others) for by in (1, -1, 0))
    far_up = shifted(opposite[low], "head", 1)
    far_down = shifted(opposite[high], "head", -1)
    near_up = shifted(above[high].astype(BF16), "head", 1)
    near_down = shifted(below[low].astype(BF16), "head", -1)
    last_up = shifted((far_up.astype(F32) + above[low]).astype(BF16), "head", 1)
    last_down = shifted(
        (far_down.astype(F32) + below[high]).astype(BF16), "head", -1
    )

    stats = jax.ShapeDtypeStruct((32, 128), F32)
    units = pltpu.VMEM((16, 128, 128), BF16)
    unit_qkv, far_probs, far_out, far_columns, far_lse = call(
        far_forward_kernel,
        (far_qkv,),
        (
            jax.ShapeDtypeStruct((3, 16, 128, 128), BF16),
            jax.ShapeDtypeStruct((16, 128, 128), F32),
            jax.ShapeDtypeStruct((128, 16, 128), BF16),
            jax.ShapeDtypeStruct((128, 128), BF16),
            stats,
        ),
        (units,),
    )
    last_up, last_down, far_out = lax.optimization_barrier(
        (last_up, last_down, far_out)
    )
    grad_rows = jnp.concatenate(
        [
            (
                here[low] + near_down.astype(F32) + last_up.astype(F32)
            ).astype(BF16),
            (
                here[high] + near_up.astype(F32) + last_down.astype(F32)
            ).astype(BF16),
        ],
        axis=0,
    )

    sent_grad, band_stats = call(
        band_kernel,
        (query_rows, key_rows, value_rows, grad_rows, far_out, far_columns),
        (jax.ShapeDtypeStruct((128, 40, 128), BF16), stats),
    )
    crossed = lax.all_to_all(sent_grad, SEQ, 0, 0, tiled=True)
    back = call(
        far_backward_kernel,
        (unit_qkv, far_probs, far_lse, crossed),
        jax.ShapeDtypeStruct((128, 48, 128), BF16),
        (units, pltpu.VMEM((3, 16, 128, 128), BF16)),
    )
    home = lax.all_to_all(back, SEQ, 0, 0, tiled=True)
    shape = jax.ShapeDtypeStruct((tokens, width), BF16)
    wide = jax.ShapeDtypeStruct((tokens, width), F32)
    attended, dq, dk, dv = call(
        band_backward_kernel,
        (query_rows, key_rows, value_rows, grad_rows, band_stats, crossed),
        (shape, wide, wide, wide),
        (units,),
    )
    grads = final_call((dq, dk, dv), home, shape)
    return (attended, *grads)


def solution(mesh):
    fine = Mesh(mesh.devices.reshape(4, 4, 4, 2, 4), ("x", "zl", "y", "core", "head"))
    rows = P(SEQ, "head")
    return jax.shard_map(
        program,
        mesh=fine,
        in_specs=(rows, rows, rows, rows, P("head", SEQ)),
        out_specs=(rows, rows, rows, rows),
        check_vma=False,
    )
```

profile of v0, /device:TPU:1, one launch (start us, length us, event | category | flops | bytes accessed | tf_op | source)
XLA Modules:
  0.0 312.3 jit_solution(4253494063286808987)
XLA Ops:
  2.2 7.1 %collective-permute-start.3 = (bf16[32,512]{1,0:T(8,128)(2,1)S(1)}, bf16[32,512]{1,0:T(8,128)(2,1)S(1)}, u32[]{:S(2)}, u32[]{:S(2)}) collective-permute-start(bf16[32,512]{1,0:T(8,128)(2,1)S(1)} %collective-permute-done), channel_id=1, source_target_pairs={{0,96},{32,0},{64,32},{96,64},{1,97},{33,1},{65,33},{97,65},{2,98}... | collective-permute-start | bytes 98312 | tf_op jit(solution)/shard_map/ppermute | solution.py:293
  13.4 4.2 %collective-permute-done.1 = bf16[32,512]{1,0:T(8,128)(2,1)S(1)} collective-permute-done((bf16[32,512]{1,0:T(8,128)(2,1)S(1)}, bf16[32,512]{1,0:T(8,128)(2,1)S(1)}, u32[]{:S(2)}, u32[]{:S(2)}) %collective-permute-start.1) | collective-permute-done | bytes 32800 | tf_op jit(solution)/shard_map/ppermute | solution.py:293
  17.7 3.2 %collective-permute-start.4 = (bf16[128,512]{1,0:T(8,128)(2,1)S(1)}, bf16[128,512]{1,0:T(8,128)(2,1)S(1)}, u32[]{:S(2)}, u32[]{:S(2)}) collective-permute-start(bf16[128,512]{1,0:T(8,128)(2,1)S(1)} %get-tuple-element.56), channel_id=1, source_target_pairs={{0,8},{8,16},{16,24},{24,0},{1,9},{9,17},{17,25},{25,1},{2,10},{10... | collective-permute-start | bytes 393224 | tf_op jit(solution)/shard_map/ppermute | solution.py:293
  20.9 4.5 %collective-permute-start.5 = (bf16[128,512]{1,0:T(8,128)(2,1)S(1)}, bf16[128,512]{1,0:T(8,128)(2,1)S(1)}, u32[]{:S(2)}, u32[]{:S(2)}) collective-permute-start(bf16[128,512]{1,0:T(8,128)(2,1)S(1)} %get-tuple-element.56), channel_id=1, source_target_pairs={{0,16},{8,24},{16,0},{24,8},{1,17},{9,25},{17,1},{25,9},{2,18},{10... | collective-permute-start | bytes 393224 | tf_op jit(solution)/shard_map/ppermute | solution.py:293
  31.8 3.0 collective-permute-start.6
  34.9 2.7 collective-permute-done.6
  37.6 27.8 %all-to-all-start = ((bf16[128,48,128]{2,1,0:T(8,128)(2,1)}), bf16[128,48,128]{2,1,0:T(8,128)(2,1)S(1)}, u32[]{:S(2)}, u32[]{:S(2)}) async-start(bf16[128,48,128]{2,1,0:T(8,128)(2,1)} %copy-done.1), calls=%async_computation | async-start | bytes 3145728 | tf_op jit(solution)/shard_map/all_to_all | solution.py:330
  65.5 5.0 %collective-permute-start.9 = (bf16[512,512]{1,0:T(8,128)(2,1)S(1)}, bf16[512,512]{1,0:T(8,128)(2,1)S(1)}, u32[]{:S(2)}, u32[]{:S(2)}) collective-permute-start(bf16[512,512]{1,0:T(8,128)(2,1)S(1)} %constant_dynamic-update-slice_fusion.4), channel_id=1, source_target_pairs={{0,384},{128,0},{256,128},{384,256},{1,385},{129,1},{257,129},{385... | collective-permute-start | bytes 1572872 | tf_op jit(solution)/shard_map/ppermute | solution.py:293
  72.5 2.7 collective-permute-start.7
  75.3 16.9 %collective-permute-done.9 = bf16[512,512]{1,0:T(8,128)(2,1)S(1)} collective-permute-done((bf16[512,512]{1,0:T(8,128)(2,1)S(1)}, bf16[512,512]{1,0:T(8,128)(2,1)S(1)}, u32[]{:S(2)}, u32[]{:S(2)}) %collective-permute-start.9) | collective-permute-done | bytes 524320 | tf_op jit(solution)/shard_map/ppermute | solution.py:293
  94.0 14.4 %collective-permute-done.7 = bf16[512,512]{1,0:T(8,128)(2,1)S(1)} collective-permute-done((bf16[512,512]{1,0:T(8,128)(2,1)S(1)}, bf16[512,512]{1,0:T(8,128)(2,1)S(1)}, u32[]{:S(2)}, u32[]{:S(2)}) %collective-permute-start.7) | collective-permute-done | bytes 524320 | tf_op jit(solution)/shard_map/ppermute | solution.py:293
  111.1 3.0 fusion.45
  118.4 8.4 %collective-permute-start.14 = (bf16[256,512]{1,0:T(8,128)(2,1)S(1)}, bf16[256,512]{1,0:T(8,128)(2,1)S(1)}, u32[]{:S(2)}, u32[]{:S(2)}) collective-permute-start(bf16[256,512]{1,0:T(8,128)(2,1)S(1)} %get-tuple-element.54), channel_id=1, source_target_pairs={{0,3},{1,0},{2,1},{3,2},{4,7},{5,4},{6,5},{7,6},{8,11},{9,8},{10,9... | collective-permute-start | bytes 786440 | tf_op jit(solution)/shard_map/ppermute | solution.py:293
  130.9 7.3 %collective-permute-start.16 = (bf16[256,512]{1,0:T(8,128)(2,1)S(1)}, bf16[256,512]{1,0:T(8,128)(2,1)S(1)}, u32[]{:S(2)}, u32[]{:S(2)}) collective-permute-start(bf16[256,512]{1,0:T(8,128)(2,1)S(1)} %slice.90), channel_id=1, source_target_pairs={{0,1},{1,2},{2,3},{3,0},{4,5},{5,6},{6,7},{7,4},{8,9},{9,10},{10,1... | collective-permute-start | bytes 786440 | tf_op jit(solution)/shard_map/ppermute | solution.py:293
  142.6 8.0 %shard_map.85 = (bf16[3,16,128,128]{3,2,1,0:T(8,128)(2,1)S(1)}, f32[16,128,128]{2,1,0:T(8,128)S(1)}, bf16[128,16,128]{2,1,0:T(8,128)(2,1)S(1)}, bf16[128,128]{1,0:T(8,128)(2,1)S(1)}, f32[32,128]{1,0:T(8,128)S(1)}) custom-call(bf16[128,48,128]{2,1,0:T(8,128)(2,1)S(1)} %all-to-all-done.qkv_ref), custom_call_target="tpu_custom_call" | custom-call | tf_op jit(solution)/shard_map/pallas_call | solution.py:282
  150.7 7.3 %collective-permute-start.13 = (bf16[256,512]{1,0:T(8,128)(2,1)S(1)}, bf16[256,512]{1,0:T(8,128)(2,1)S(1)}, u32[]{:S(2)}, u32[]{:S(2)}) collective-permute-start(bf16[256,512]{1,0:T(8,128)(2,1)S(1)} %fusion.52), channel_id=1, source_target_pairs={{0,1},{1,2},{2,3},{3,0},{4,5},{5,6},{6,7},{7,4},{8,9},{9,10},{10,1... | collective-permute-start | bytes 786440 | tf_op jit(solution)/shard_map/ppermute | solution.py:293
  161.5 37.9 %collective-permute-done.13 = bf16[256,512]{1,0:T(8,128)(2,1)S(1)} collective-permute-done((bf16[256,512]{1,0:T(8,128)(2,1)S(1)}, bf16[256,512]{1,0:T(8,128)(2,1)S(1)}, u32[]{:S(2)}, u32[]{:S(2)}) %collective-permute-start.13) | collective-permute-done | bytes 262176 | tf_op jit(solution)/shard_map/ppermute | solution.py:293
  199.7 2.7 shard_map.86
  202.5 47.7 %all_to_all.15.far_ref.g_ref = bf16[128,40,128]{2,1,0:T(8,128)(2,1)S(1)} all-to-all(bf16[128,40,128]{2,1,0:T(8,128)(2,1)S(1)} %get-tuple-element.41), channel_id=1, replica_groups=mesh['x'=4,'zl'=4,'y'=4,'core'=2,'head'=4] {'x','zl','y','core'}, dimensions={0} | all-to-all | bytes 2621440 | tf_op jit(solution)/shard_map/all_to_all | solution.py:394
  250.2 7.8 %shard_map.88 = bf16[128,48,128]{2,1,0:T(8,128)(2,1)S(1)} custom-call(bf16[3,16,128,128]{3,2,1,0:T(8,128)(2,1)S(1)} %get-tuple-element.46.unit_ref, f32[16,128,128]{2,1,0:T(8,128)S(1)} %get-tuple-element.47.probs_ref, f32[32,128]{1,0:T(8,128)S(1)} %get-tuple-element.48.lse_ref, bf16[128,40,128]{2,1,0:T(8,128)(2,1)S(1)} %all_to_all.15.far_ref.g_ref), custom_call_target="tpu_custom_call" | custom-call | tf_op jit(solution)/shard_map/pallas_call | solution.py:282
  259.2 7.5 %all-to-all-start.2 = ((bf16[128,48,128]{2,1,0:T(8,128)(2,1)}), bf16[128,48,128]{2,1,0:T(8,128)(2,1)}, u32[]{:S(2)}, u32[]{:S(2)}) async-start(bf16[128,48,128]{2,1,0:T(8,128)(2,1)} %copy-done.2), calls=%async_computation.2 | async-start | bytes 3145728 | tf_op jit(solution)/shard_map/all_to_all | solution.py:401
  269.8 6.8 %shard_map.87 = (bf16[512,512]{1,0:T(8,128)(2,1)}, f32[512,512]{1,0:T(8,128)S(1)}, f32[512,512]{1,0:T(8,128)S(1)}, f32[512,512]{1,0:T(8,128)S(1)}) custom-call(bf16[512,512]{1,0:T(8,128)(2,1)S(1)} %copy-done.5, bf16[512,512]{1,0:T(8,128)(2,1)S(1)} %copy-done.8, bf16[512,512]{1,0:T(8,128)(2,1)S(1)} %copy-done.11, ...), custom_call_target="tpu_custom_call" | custom-call | tf_op jit(solution)/shard_map/pallas_call | solution.py:282
  279.5 27.6 %all-to-all-done.2.far_ref = bf16[128,48,128]{2,1,0:T(8,128)(2,1)} async-done(((bf16[128,48,128]{2,1,0:T(8,128)(2,1)}), bf16[128,48,128]{2,1,0:T(8,128)(2,1)}, u32[]{:S(2)}, u32[]{:S(2)}) %all-to-all-start.2) | async-done | bytes 1572896 | tf_op jit(solution)/shard_map/all_to_all | solution.py:401
  307.1 5.2 %shard_map.89 = (bf16[512,512]{1,0:T(8,128)(2,1)}, bf16[512,512]{1,0:T(8,128)(2,1)}, bf16[512,512]{1,0:T(8,128)(2,1)}) custom-call(f32[512,512]{1,0:T(8,128)} %copy-done.12, f32[512,512]{1,0:T(8,128)} %copy-done.13, f32[512,512]{1,0:T(8,128)} %copy-done.14, bf16[128,48,128]{2,1,0:T(8,128)(2,1)} %all-to-all-done.2.far_ref), custom_call_target="tpu_custom_call" | custom-call | tf_op jit(solution)/shard_map/pallas_call | solution.py:269
  (87 shorter events, 42.3 us)
Async XLA Ops:
  0.6 110.4 %copy-start = (bf16[512,1024]{1,0:T(8,128)(2,1)S(1)}, bf16[512,1024]{1,0:T(8,128)(2,1)}, u32[]{:S(2)}) copy-start(bf16[512,1024]{1,0:T(8,128)(2,1)} %param.8) | copy-start | bytes 3145732
  0.6 1.6 collective-permute-start
  2.2 15.5 %collective-permute-start.3 = (bf16[32,512]{1,0:T(8,128)(2,1)S(1)}, bf16[32,512]{1,0:T(8,128)(2,1)S(1)}, u32[]{:S(2)}, u32[]{:S(2)}) collective-permute-start(bf16[32,512]{1,0:T(8,128)(2,1)S(1)} %collective-permute-done), channel_id=1, source_target_pairs={{0,96},{32,0},{64,32},{96,64},{1,97},{33,1},{65,33},{97,65},{2,98}... | collective-permute-start | bytes 98312 | tf_op jit(solution)/shard_map/ppermute | solution.py:293
  9.3 8.4 %collective-permute-start.2 = (bf16[32,512]{1,0:T(8,128)(2,1)S(1)}, bf16[32,512]{1,0:T(8,128)(2,1)S(1)}, u32[]{:S(2)}, u32[]{:S(2)}) collective-permute-start(bf16[32,512]{1,0:T(8,128)(2,1)S(1)} %collective-permute-done), channel_id=1, source_target_pairs={{0,64},{32,96},{64,0},{96,32},{1,65},{33,97},{65,1},{97,33},{2,66}... | collective-permute-start | bytes 98312 | tf_op jit(solution)/shard_map/ppermute | solution.py:293
  11.2 6.5 %collective-permute-start.1 = (bf16[32,512]{1,0:T(8,128)(2,1)S(1)}, bf16[32,512]{1,0:T(8,128)(2,1)S(1)}, u32[]{:S(2)}, u32[]{:S(2)}) collective-permute-start(bf16[32,512]{1,0:T(8,128)(2,1)S(1)} %collective-permute-done), channel_id=1, source_target_pairs={{0,32},{32,64},{64,96},{96,0},{1,33},{33,65},{65,97},{97,1},{2,34}... | collective-permute-start | bytes 98312 | tf_op jit(solution)/shard_map/ppermute | solution.py:293
  17.7 17.1 %collective-permute-start.4 = (bf16[128,512]{1,0:T(8,128)(2,1)S(1)}, bf16[128,512]{1,0:T(8,128)(2,1)S(1)}, u32[]{:S(2)}, u32[]{:S(2)}) collective-permute-start(bf16[128,512]{1,0:T(8,128)(2,1)S(1)} %get-tuple-element.56), channel_id=1, source_target_pairs={{0,8},{8,16},{16,24},{24,0},{1,9},{9,17},{17,25},{25,1},{2,10},{10... | collective-permute-start | bytes 393224 | tf_op jit(solution)/shard_map/ppermute | solution.py:293
  20.9 13.9 %collective-permute-start.5 = (bf16[128,512]{1,0:T(8,128)(2,1)S(1)}, bf16[128,512]{1,0:T(8,128)(2,1)S(1)}, u32[]{:S(2)}, u32[]{:S(2)}) collective-permute-start(bf16[128,512]{1,0:T(8,128)(2,1)S(1)} %get-tuple-element.56), channel_id=1, source_target_pairs={{0,16},{8,24},{16,0},{24,8},{1,17},{9,25},{17,1},{25,9},{2,18},{10... | collective-permute-start | bytes 393224 | tf_op jit(solution)/shard_map/ppermute | solution.py:293
  31.8 5.7 %collective-permute-start.6 = (bf16[128,512]{1,0:T(8,128)(2,1)S(1)}, bf16[128,512]{1,0:T(8,128)(2,1)S(1)}, u32[]{:S(2)}, u32[]{:S(2)}) collective-permute-start(bf16[128,512]{1,0:T(8,128)(2,1)S(1)} %get-tuple-element.56), channel_id=1, source_target_pairs={{0,24},{8,0},{16,8},{24,16},{1,25},{9,1},{17,9},{25,17},{2,26},{10... | collective-permute-start | bytes 393224 | tf_op jit(solution)/shard_map/ppermute | solution.py:293
  37.6 77.4 %all-to-all-start = ((bf16[128,48,128]{2,1,0:T(8,128)(2,1)}), bf16[128,48,128]{2,1,0:T(8,128)(2,1)S(1)}, u32[]{:S(2)}, u32[]{:S(2)}) async-start(bf16[128,48,128]{2,1,0:T(8,128)(2,1)} %copy-done.1), calls=%async_computation | async-start | bytes 3145728 | tf_op jit(solution)/shard_map/all_to_all | solution.py:330
  65.5 26.8 %collective-permute-start.9 = (bf16[512,512]{1,0:T(8,128)(2,1)S(1)}, bf16[512,512]{1,0:T(8,128)(2,1)S(1)}, u32[]{:S(2)}, u32[]{:S(2)}) collective-permute-start(bf16[512,512]{1,0:T(8,128)(2,1)S(1)} %constant_dynamic-update-slice_fusion.4), channel_id=1, source_target_pairs={{0,384},{128,0},{256,128},{384,256},{1,385},{129,1},{257,129},{385... | collective-permute-start | bytes 1572872 | tf_op jit(solution)/shard_map/ppermute | solution.py:293
  70.5 23.6 %collective-permute-start.8 = (bf16[512,512]{1,0:T(8,128)(2,1)S(1)}, bf16[512,512]{1,0:T(8,128)(2,1)S(1)}, u32[]{:S(2)}, u32[]{:S(2)}) collective-permute-start(bf16[512,512]{1,0:T(8,128)(2,1)S(1)} %constant_dynamic-update-slice_fusion.4), channel_id=1, source_target_pairs={{0,256},{128,384},{256,0},{384,128},{1,257},{129,385},{257,1},{385... | collective-permute-start | bytes 1572872 | tf_op jit(solution)/shard_map/ppermute | solution.py:293
  72.5 35.9 %collective-permute-start.7 = (bf16[512,512]{1,0:T(8,128)(2,1)S(1)}, bf16[512,512]{1,0:T(8,128)(2,1)S(1)}, u32[]{:S(2)}, u32[]{:S(2)}) collective-permute-start(bf16[512,512]{1,0:T(8,128)(2,1)S(1)} %constant_dynamic-update-slice_fusion.4), channel_id=1, source_target_pairs={{0,128},{128,256},{256,384},{384,0},{1,129},{129,257},{257,385},{3... | collective-permute-start | bytes 1572872 | tf_op jit(solution)/shard_map/ppermute | solution.py:293
  108.7 6.2 %collective-permute-start.10 = (bf16[4,512,512]{2,1,0:T(8,128)(2,1)S(1)}, bf16[4,512,512]{2,1,0:T(8,128)(2,1)}, u32[]{:S(2)}, u32[]{:S(2)}) collective-permute-start(bf16[4,512,512]{2,1,0:T(8,128)(2,1)S(1)} %pad_maximum_fusion), channel_id=1, source_target_pairs={{0,4},{4,0},{1,5},{5,1},{2,6},{6,2},{3,7},{7,3},{8,12},{12,8},{9,1... | collective-permute-start | bytes 6291464 | tf_op jit(solution)/shard_map/ppermute | solution.py:332
  116.7 12.1 %copy-start.17 = (bf16[4,512,512]{2,1,0:T(8,128)(2,1)S(1)}, bf16[4,512,512]{2,1,0:T(8,128)(2,1)}, u32[]{:S(2)}) copy-start(bf16[4,512,512]{2,1,0:T(8,128)(2,1)} %copy-done.16) | copy-start | bytes 6291460
  118.4 39.5 %collective-permute-start.14 = (bf16[256,512]{1,0:T(8,128)(2,1)S(1)}, bf16[256,512]{1,0:T(8,128)(2,1)S(1)}, u32[]{:S(2)}, u32[]{:S(2)}) collective-permute-start(bf16[256,512]{1,0:T(8,128)(2,1)S(1)} %get-tuple-element.54), channel_id=1, source_target_pairs={{0,3},{1,0},{2,1},{3,2},{4,7},{5,4},{6,5},{7,6},{8,11},{9,8},{10,9... | collective-permute-start | bytes 786440 | tf_op jit(solution)/shard_map/ppermute | solution.py:293
  126.9 23.7 %collective-permute-start.12 = (bf16[256,512]{1,0:T(8,128)(2,1)S(1)}, bf16[256,512]{1,0:T(8,128)(2,1)S(1)}, u32[]{:S(2)}, u32[]{:S(2)}) collective-permute-start(bf16[256,512]{1,0:T(8,128)(2,1)S(1)} %get-tuple-element.55), channel_id=1, source_target_pairs={{0,1},{1,2},{2,3},{3,0},{4,5},{5,6},{6,7},{7,4},{8,9},{9,10},{10,1... | collective-permute-start | bytes 786440 | tf_op jit(solution)/shard_map/ppermute | solution.py:293
  130.9 68.5 %collective-permute-start.16 = (bf16[256,512]{1,0:T(8,128)(2,1)S(1)}, bf16[256,512]{1,0:T(8,128)(2,1)S(1)}, u32[]{:S(2)}, u32[]{:S(2)}) collective-permute-start(bf16[256,512]{1,0:T(8,128)(2,1)S(1)} %slice.90), channel_id=1, source_target_pairs={{0,1},{1,2},{2,3},{3,0},{4,5},{5,6},{6,7},{7,4},{8,9},{9,10},{10,1... | collective-permute-start | bytes 786440 | tf_op jit(solution)/shard_map/ppermute | solution.py:293
  140.6 58.8 %collective-permute-start.11 = (bf16[256,512]{1,0:T(8,128)(2,1)S(1)}, bf16[256,512]{1,0:T(8,128)(2,1)S(1)}, u32[]{:S(2)}, u32[]{:S(2)}) collective-permute-start(bf16[256,512]{1,0:T(8,128)(2,1)S(1)} %slice.91), channel_id=1, source_target_pairs={{0,3},{1,0},{2,1},{3,2},{4,7},{5,4},{6,5},{7,6},{8,11},{9,8},{10,9... | collective-permute-start | bytes 786440 | tf_op jit(solution)/shard_map/ppermute | solution.py:293
  150.7 48.7 %collective-permute-start.13 = (bf16[256,512]{1,0:T(8,128)(2,1)S(1)}, bf16[256,512]{1,0:T(8,128)(2,1)S(1)}, u32[]{:S(2)}, u32[]{:S(2)}) collective-permute-start(bf16[256,512]{1,0:T(8,128)(2,1)S(1)} %fusion.52), channel_id=1, source_target_pairs={{0,1},{1,2},{2,3},{3,0},{4,5},{5,6},{6,7},{7,4},{8,9},{9,10},{10,1... | collective-permute-start | bytes 786440 | tf_op jit(solution)/shard_map/ppermute | solution.py:293
  158.0 41.4 %collective-permute-start.15 = (bf16[256,512]{1,0:T(8,128)(2,1)S(1)}, bf16[256,512]{1,0:T(8,128)(2,1)S(1)}, u32[]{:S(2)}, u32[]{:S(2)}) collective-permute-start(bf16[256,512]{1,0:T(8,128)(2,1)S(1)} %fusion.51), channel_id=1, source_target_pairs={{0,3},{1,0},{2,1},{3,2},{4,7},{5,4},{6,5},{7,6},{8,11},{9,8},{10,9... | collective-permute-start | bytes 786440 | tf_op jit(solution)/shard_map/ppermute | solution.py:293
  161.5 38.2 %copy-start.4 = (bf16[512,512]{1,0:T(8,128)(2,1)S(1)}, bf16[512,512]{1,0:T(8,128)(2,1)}, u32[]{:S(2)}) copy-start(bf16[512,512]{1,0:T(8,128)(2,1)} %q_ref.5) | copy-start | bytes 1572868
  161.5 38.2 %copy-start.7 = (bf16[512,512]{1,0:T(8,128)(2,1)S(1)}, bf16[512,512]{1,0:T(8,128)(2,1)}, u32[]{:S(2)}) copy-start(bf16[512,512]{1,0:T(8,128)(2,1)} %k_ref.5) | copy-start | bytes 1572868
  161.5 38.2 %copy-start.10 = (bf16[512,512]{1,0:T(8,128)(2,1)S(1)}, bf16[512,512]{1,0:T(8,128)(2,1)}, u32[]{:S(2)}) copy-start(bf16[512,512]{1,0:T(8,128)(2,1)} %v_ref.5) | copy-start | bytes 1572868
  259.2 47.9 %all-to-all-start.2 = ((bf16[128,48,128]{2,1,0:T(8,128)(2,1)}), bf16[128,48,128]{2,1,0:T(8,128)(2,1)}, u32[]{:S(2)}, u32[]{:S(2)}) async-start(bf16[128,48,128]{2,1,0:T(8,128)(2,1)} %copy-done.2), calls=%async_computation.2 | async-start | bytes 3145728 | tf_op jit(solution)/shard_map/all_to_all | solution.py:401
  (13 other events, 18.7 us)
where the time goes:
time: 314 us; the launch traced here: 312 us
  waiting for transfers between devices  106 us (34%)
  starting transfers between devices  99.5 us (32%)
  blocking collectives  47.7 us (15%)
  Pallas kernels  32.6 us (10%)
  matrix products  12.4 us (4%)
  local copies, waits for them, and re-layouts  11.7 us (4%)
    ppermute x15, waiting for transfers between devices, shifted(): return lax.ppermute(values, axis, [(i, (i + by) % 4) for i in range(4)])  78 us
    ppermute x15, starting transfers between devices, shifted(): return lax.ppermute(values, axis, [(i, (i + by) % 4) for i in range(4)])  60.4 us
    all_to_all x1, blocking collectives, program(): crossed = lax.all_to_all(sent_grad, SEQ, 0, 0, tiled=True)  47.7 us
    all_to_all x1, starting transfers between devices, program(): far_qkv = lax.all_to_all(sent, SEQ, 0, 0, tiled=True)  27.8 us
    all_to_all x1, waiting for transfers between devices, program(): home = lax.all_to_all(back, SEQ, 0, 0, tiled=True)  27.6 us
    pallas_call x5, Pallas kernels, call(): pl.pallas_call(kernel, out_shape=outs, in_specs=[vmem] * len(args), out_s...  27.4 us
    unnamed x41, local copies, waits for them, and re-layouts  11.6 us
    all_to_all x1, starting transfers between devices, program(): home = lax.all_to_all(back, SEQ, 0, 0, tiled=True)  7.45 us
  transfers between devices with their start and end apart: 19, of which 8 were waited for; matrix products, arithmetic and copies ran while one was open for 3% of the time, Pallas kernels for 5%

commit v1 on v0

--- a/solution.py
+++ b/solution.py
@@ -86,7 +86,29 @@
 
 
 def pack_kernel(q_ref, k_ref, v_ref, out_ref):
-    pack_rows((q_ref, k_ref, v_ref), out_ref)
+    swap = swap_matrix()
+    for block in range(2):
+        place = slice(block * 16, block * 16 + 16)
+        for which, source in enumerate((q_ref, k_ref, v_ref)):
+            pieces = [
+                source[unit // 4, place, (unit % 4) * 128 : (unit % 4) * 128 + 128]
+                for unit in range(UNITS)
+            ]
+            moved = nn(swap, jnp.concatenate(pieces, axis=0)).astype(BF16)
+            out_ref[place, which * 16 : which * 16 + 16, :] = moved.reshape(16, 16, 128)
+
+
+def pack_call(arrays):
+    rows = pl.BlockSpec((4, 32, arrays[0].shape[1]), lambda step: (0, step, 0))
+    split = [array.reshape(4, 128, array.shape[1]) for array in arrays]
+    return pl.pallas_call(
+        pack_kernel,
+        grid=(4,),
+        out_shape=jax.ShapeDtypeStruct((128, 48, 128), BF16),
+        in_specs=[rows] * 3,
+        out_specs=pl.BlockSpec((32, 48, 128), lambda step: (step, 0, 0)),
+        compiler_params=pltpu.CompilerParams(vmem_limit_bytes=16 * 1024 * 1024),
+    )(*[pltpu.with_memory_space_constraint(array, pltpu.HBM) for array in split])
 
 
 def masks(strict):
@@ -314,11 +336,7 @@
     tokens, width = query_rows.shape
     x, head = lax.axis_index("x"), lax.axis_index("head")
 
-    sent = call(
-        pack_kernel,
-        (query_rows, key_rows, value_rows),
-        jax.ShapeDtypeStruct((128, 48, 128), BF16),
-    )
+    sent = pack_call((query_rows, key_rows, value_rows))
     own = out_weight.T
     weight = lax.ppermute(
         own,
@@ -326,13 +344,11 @@
         [(a * 4 + h, h * 4 + a) for a in range(4) for h in range(4)],
     )
     weight = around(around(weight, "zl"), "y")
-    sent, weight = lax.optimization_barrier((sent, weight))
+    mine = jnp.stack([weight] + [shifted(weight, "x", by) for by in (1, 2, 3)])
     far_qkv = lax.all_to_all(sent, SEQ, 0, 0, tiled=True)
-    mine = jnp.stack([weight] + [shifted(weight, "x", by) for by in (1, 2, 3)])
     others = lax.ppermute(mine, "core", [(0, 1), (1, 0)])
     ordered = jnp.dot(out_grad, column_order(out_grad.shape[1]), preferred_element_type=F32)
     ordered = ordered.astype(BF16)
-    far_qkv, others = lax.optimization_barrier((far_qkv, others))
 
     def partial(target, mine, others):
         at = (x - target + 8) % 4

time: 314 us -> 312 us (level)
  matrix products: 12.4 us -> 6.86 us
    dot_general x4, matrix products: 6.28 us -> 2.82 us  [partial(): jnp.dot(ordered[:, 512:], other, preferred_element_type=F32)]
    pallas_call x0 -> x1, Pallas kernels: none -> 3.24 us  [pack_call(): pl.pallas_call(pack_kernel, grid=(4,), out_shape=jax.ShapeDtypeStruct((12...]
    unnamed x41 -> x31, local copies, waits for them, and re-layouts: 11.6 us -> 8.46 us
    pallas_call x5 -> x4, Pallas kernels: 27.4 us -> 25.4 us  [call(): pl.pallas_call(kernel, out_shape=outs, in_specs=[vmem] * len(args), out_s...]
  transfers between devices with their start and end apart: 19 -> 19, of which waited for: 8 -> 11; matrix products, arithmetic and copies ran while one was open for 3% -> 3% of each run, Pallas kernels for 5% -> 6%
where the time goes in v1:
time: 312 us; the launch traced here: 311 us
  waiting for transfers between devices  107 us (34%)
  starting transfers between devices  101 us (32%)
  blocking collectives  48.2 us (15%)
  Pallas kernels  33.8 us (11%)
  local copies, waits for them, and re-layouts  9.98 us (3%)
  matrix products  6.86 us (2%)
    ppermute x15, waiting for transfers between devices, shifted(): return lax.ppermute(values, axis, [(i, (i + by) % 4) for i in range(4)])  77.7 us
    ppermute x15, starting transfers between devices, shifted(): return lax.ppermute(values, axis, [(i, (i + by) % 4) for i in range(4)])  61.3 us
    all_to_all x1, blocking collectives, program(): crossed = lax.all_to_all(sent_grad, SEQ, 0, 0, tiled=True)  48.2 us
    all_to_all x1, starting transfers between devices, program(): far_qkv = lax.all_to_all(sent, SEQ, 0, 0, tiled=True)  28.7 us
    all_to_all x1, waiting for transfers between devices, program(): home = lax.all_to_all(back, SEQ, 0, 0, tiled=True)  27.6 us
    pallas_call x4, Pallas kernels, call(): pl.pallas_call(kernel, out_shape=outs, in_specs=[vmem] * len(args), out_s...  25.4 us
    unnamed x31, local copies, waits for them, and re-layouts  8.46 us
    all_to_all x1, starting transfers between devices, program(): home = lax.all_to_all(back, SEQ, 0, 0, tiled=True)  7.45 us
  transfers between devices with their start and end apart: 19, of which 11 were waited for; matrix products, arithmetic and copies ran while one was open for 3% of the time, Pallas kernels for 6%

profile of v1, /device:TPU:1, one launch (start us, length us, event | category | flops | bytes accessed | tf_op | source)
XLA Modules:
  0.0 311.3 jit_solution(1752504380838821497)
XLA Ops:
  2.2 4.4 %collective-permute-start.1 = (bf16[32,512]{1,0:T(8,128)(2,1)S(1)}, bf16[32,512]{1,0:T(8,128)(2,1)S(1)}, u32[]{:S(2)}, u32[]{:S(2)}) collective-permute-start(bf16[32,512]{1,0:T(8,128)(2,1)S(1)} %collective-permute-done), channel_id=1, source_target_pairs={{0,32},{32,64},{64,96},{96,0},{1,33},{33,65},{65,97},{97,1},{2,34}... | collective-permute-start | bytes 98312 | tf_op jit(solution)/shard_map/ppermute | solution.py:315
  6.6 4.9 %collective-permute-start.2 = (bf16[32,512]{1,0:T(8,128)(2,1)S(1)}, bf16[32,512]{1,0:T(8,128)(2,1)S(1)}, u32[]{:S(2)}, u32[]{:S(2)}) collective-permute-start(bf16[32,512]{1,0:T(8,128)(2,1)S(1)} %collective-permute-done), channel_id=1, source_target_pairs={{0,64},{32,96},{64,0},{96,32},{1,65},{33,97},{65,1},{97,33},{2,66}... | collective-permute-start | bytes 98312 | tf_op jit(solution)/shard_map/ppermute | solution.py:315
  23.8 28.7 %all-to-all-start = ((bf16[128,48,128]{2,1,0:T(8,128)(2,1)}), bf16[128,48,128]{2,1,0:T(8,128)(2,1)S(1)}, u32[]{:S(2)}, u32[]{:S(2)}) async-start(bf16[128,48,128]{2,1,0:T(8,128)(2,1)} %copy-done.1), calls=%async_computation | async-start | bytes 3145728 | tf_op jit(solution)/shard_map/all_to_all | solution.py:348
  52.5 4.8 %collective-permute-start.5 = (bf16[128,512]{1,0:T(8,128)(2,1)S(1)}, bf16[128,512]{1,0:T(8,128)(2,1)S(1)}, u32[]{:S(2)}, u32[]{:S(2)}) collective-permute-start(bf16[128,512]{1,0:T(8,128)(2,1)S(1)} %get-tuple-element.48), channel_id=1, source_target_pairs={{0,16},{8,24},{16,0},{24,8},{1,17},{9,25},{17,1},{25,9},{2,18},{10... | collective-permute-start | bytes 393224 | tf_op jit(solution)/shard_map/ppermute | solution.py:315
  60.1 8.8 %collective-permute-done.5 = bf16[128,512]{1,0:T(8,128)(2,1)S(1)} collective-permute-done((bf16[128,512]{1,0:T(8,128)(2,1)S(1)}, bf16[128,512]{1,0:T(8,128)(2,1)S(1)}, u32[]{:S(2)}, u32[]{:S(2)}) %collective-permute-start.5) | collective-permute-done | bytes 131104 | tf_op jit(solution)/shard_map/ppermute | solution.py:315
  69.0 4.6 %collective-permute-done.6 = bf16[128,512]{1,0:T(8,128)(2,1)S(1)} collective-permute-done((bf16[128,512]{1,0:T(8,128)(2,1)S(1)}, bf16[128,512]{1,0:T(8,128)(2,1)S(1)}, u32[]{:S(2)}, u32[]{:S(2)}) %collective-permute-start.6) | collective-permute-done | bytes 131104 | tf_op jit(solution)/shard_map/ppermute | solution.py:315
  73.6 3.6 %collective-permute-start.9 = (bf16[512,512]{1,0:T(8,128)(2,1)S(1)}, bf16[512,512]{1,0:T(8,128)(2,1)S(1)}, u32[]{:S(2)}, u32[]{:S(2)}) collective-permute-start(bf16[512,512]{1,0:T(8,128)(2,1)S(1)} %constant_dynamic-update-slice_fusion.4), channel_id=1, source_target_pairs={{0,384},{128,0},{256,128},{384,256},{1,385},{129,1},{257,129},{385... | collective-permute-start | bytes 1572872 | tf_op jit(solution)/shard_map/ppermute | solution.py:315
  77.1 3.4 %collective-permute-start.8 = (bf16[512,512]{1,0:T(8,128)(2,1)S(1)}, bf16[512,512]{1,0:T(8,128)(2,1)S(1)}, u32[]{:S(2)}, u32[]{:S(2)}) collective-permute-start(bf16[512,512]{1,0:T(8,128)(2,1)S(1)} %constant_dynamic-update-slice_fusion.4), channel_id=1, source_target_pairs={{0,256},{128,384},{256,0},{384,128},{1,257},{129,385},{257,1},{385... | collective-permute-start | bytes 1572872 | tf_op jit(solution)/shard_map/ppermute | solution.py:315
  82.5 8.9 %collective-permute-done.9 = bf16[512,512]{1,0:T(8,128)(2,1)S(1)} collective-permute-done((bf16[512,512]{1,0:T(8,128)(2,1)S(1)}, bf16[512,512]{1,0:T(8,128)(2,1)S(1)}, u32[]{:S(2)}, u32[]{:S(2)}) %collective-permute-start.9) | collective-permute-done | bytes 524320 | tf_op jit(solution)/shard_map/ppermute | solution.py:315
  91.4 3.7 %collective-permute-done.8 = bf16[512,512]{1,0:T(8,128)(2,1)S(1)} collective-permute-done((bf16[512,512]{1,0:T(8,128)(2,1)S(1)}, bf16[512,512]{1,0:T(8,128)(2,1)S(1)}, u32[]{:S(2)}, u32[]{:S(2)}) %collective-permute-start.8) | collective-permute-done | bytes 524320 | tf_op jit(solution)/shard_map/ppermute | solution.py:315
  95.1 12.6 %collective-permute-done.7 = bf16[512,512]{1,0:T(8,128)(2,1)S(1)} collective-permute-done((bf16[512,512]{1,0:T(8,128)(2,1)S(1)}, bf16[512,512]{1,0:T(8,128)(2,1)S(1)}, u32[]{:S(2)}, u32[]{:S(2)}) %collective-permute-start.7) | collective-permute-done | bytes 524320 | tf_op jit(solution)/shard_map/ppermute | solution.py:315
  115.2 8.5 %collective-permute-start.12 = (bf16[256,512]{1,0:T(8,128)(2,1)S(1)}, bf16[256,512]{1,0:T(8,128)(2,1)S(1)}, u32[]{:S(2)}, u32[]{:S(2)}) collective-permute-start(bf16[256,512]{1,0:T(8,128)(2,1)S(1)} %get-tuple-element.47), channel_id=1, source_target_pairs={{0,1},{1,2},{2,3},{3,0},{4,5},{5,6},{6,7},{7,4},{8,9},{9,10},{10,1... | collective-permute-start | bytes 786440 | tf_op jit(solution)/shard_map/ppermute | solution.py:315
  129.4 7.3 %collective-permute-start.11 = (bf16[256,512]{1,0:T(8,128)(2,1)}, bf16[256,512]{1,0:T(8,128)(2,1)S(1)}, u32[]{:S(2)}, u32[]{:S(2)}) collective-permute-start(bf16[256,512]{1,0:T(8,128)(2,1)} %slice.91), channel_id=1, source_target_pairs={{0,3},{1,0},{2,1},{3,2},{4,7},{5,4},{6,5},{7,6},{8,11},{9,8},{10,9... | collective-permute-start | bytes 786440 | tf_op jit(solution)/shard_map/ppermute | solution.py:315
  140.1 6.6 %collective-permute-start.13 = (bf16[256,512]{1,0:T(8,128)(2,1)}, bf16[256,512]{1,0:T(8,128)(2,1)S(1)}, u32[]{:S(2)}, u32[]{:S(2)}) collective-permute-start(bf16[256,512]{1,0:T(8,128)(2,1)} %fusion.51), channel_id=1, source_target_pairs={{0,1},{1,2},{2,3},{3,0},{4,5},{5,6},{6,7},{7,4},{8,9},{9,10},{10,1... | collective-permute-start | bytes 786440 | tf_op jit(solution)/shard_map/ppermute | solution.py:315
  146.7 21.0 %collective-permute-done.14 = bf16[256,512]{1,0:T(8,128)(2,1)S(1)} collective-permute-done((bf16[256,512]{1,0:T(8,128)(2,1)S(1)}, bf16[256,512]{1,0:T(8,128)(2,1)S(1)}, u32[]{:S(2)}, u32[]{:S(2)}) %collective-permute-start.14) | collective-permute-done | bytes 262176 | tf_op jit(solution)/shard_map/ppermute | solution.py:315
  173.2 8.0 %shard_map.85 = (bf16[3,16,128,128]{3,2,1,0:T(8,128)(2,1)S(1)}, f32[16,128,128]{2,1,0:T(8,128)S(1)}, bf16[128,16,128]{2,1,0:T(8,128)(2,1)S(1)}, bf16[128,128]{1,0:T(8,128)(2,1)S(1)}, f32[32,128]{1,0:T(8,128)S(1)}) custom-call(bf16[128,48,128]{2,1,0:T(8,128)(2,1)S(1)} %all-to-all-done.qkv_ref), custom_call_target="tpu_custom_call" | custom-call | tf_op jit(solution)/shard_map/pallas_call | solution.py:304
  181.3 7.2 %collective-permute-done.13 = bf16[256,512]{1,0:T(8,128)(2,1)S(1)} collective-permute-done((bf16[256,512]{1,0:T(8,128)(2,1)}, bf16[256,512]{1,0:T(8,128)(2,1)S(1)}, u32[]{:S(2)}, u32[]{:S(2)}) %collective-permute-start.13) | collective-permute-done | bytes 262176 | tf_op jit(solution)/shard_map/ppermute | solution.py:315
  188.5 8.5 %collective-permute-done.15 = bf16[256,512]{1,0:T(8,128)(2,1)} collective-permute-done((bf16[256,512]{1,0:T(8,128)(2,1)}, bf16[256,512]{1,0:T(8,128)(2,1)}, u32[]{:S(2)}, u32[]{:S(2)}) %collective-permute-start.15) | collective-permute-done | bytes 262176 | tf_op jit(solution)/shard_map/ppermute | solution.py:315
  201.0 48.2 %all_to_all.15.far_ref.g_ref = bf16[128,40,128]{2,1,0:T(8,128)(2,1)S(1)} all-to-all(bf16[128,40,128]{2,1,0:T(8,128)(2,1)S(1)} %get-tuple-element.33), channel_id=1, replica_groups=mesh['x'=4,'zl'=4,'y'=4,'core'=2,'head'=4] {'x','zl','y','core'}, dimensions={0} | all-to-all | bytes 2621440 | tf_op jit(solution)/shard_map/all_to_all | solution.py:410
  249.2 7.8 %shard_map.88 = bf16[128,48,128]{2,1,0:T(8,128)(2,1)S(1)} custom-call(bf16[3,16,128,128]{3,2,1,0:T(8,128)(2,1)S(1)} %get-tuple-element.38.unit_ref, f32[16,128,128]{2,1,0:T(8,128)S(1)} %get-tuple-element.39.probs_ref, f32[32,128]{1,0:T(8,128)S(1)} %get-tuple-element.40.lse_ref, bf16[128,40,128]{2,1,0:T(8,128)(2,1)S(1)} %all_to_all.15.far_ref.g_ref), custom_call_target="tpu_custom_call" | custom-call | tf_op jit(solution)/shard_map/pallas_call | solution.py:304
  258.2 7.5 %all-to-all-start.2 = ((bf16[128,48,128]{2,1,0:T(8,128)(2,1)}), bf16[128,48,128]{2,1,0:T(8,128)(2,1)}, u32[]{:S(2)}, u32[]{:S(2)}) async-start(bf16[128,48,128]{2,1,0:T(8,128)(2,1)} %copy-done.2), calls=%async_computation.2 | async-start | bytes 3145728 | tf_op jit(solution)/shard_map/all_to_all | solution.py:417
  268.8 6.8 %shard_map.87 = (bf16[512,512]{1,0:T(8,128)(2,1)}, f32[512,512]{1,0:T(8,128)S(1)}, f32[512,512]{1,0:T(8,128)S(1)}, f32[512,512]{1,0:T(8,128)S(1)}) custom-call(bf16[512,512]{1,0:T(8,128)(2,1)S(1)} %copy-done.4, bf16[512,512]{1,0:T(8,128)(2,1)S(1)} %copy-done.6, bf16[512,512]{1,0:T(8,128)(2,1)S(1)} %copy-done.8, ...), custom_call_target="tpu_custom_call" | custom-call | tf_op jit(solution)/shard_map/pallas_call | solution.py:304
  278.5 27.6 %all-to-all-done.2.far_ref = bf16[128,48,128]{2,1,0:T(8,128)(2,1)} async-done(((bf16[128,48,128]{2,1,0:T(8,128)(2,1)}), bf16[128,48,128]{2,1,0:T(8,128)(2,1)}, u32[]{:S(2)}, u32[]{:S(2)}) %all-to-all-start.2) | async-done | bytes 1572896 | tf_op jit(solution)/shard_map/all_to_all | solution.py:417
  306.1 5.2 %shard_map.89 = (bf16[512,512]{1,0:T(8,128)(2,1)}, bf16[512,512]{1,0:T(8,128)(2,1)}, bf16[512,512]{1,0:T(8,128)(2,1)}) custom-call(f32[512,512]{1,0:T(8,128)} %copy-done.9, f32[512,512]{1,0:T(8,128)} %copy-done.10, f32[512,512]{1,0:T(8,128)} %copy-done.11, bf16[128,48,128]{2,1,0:T(8,128)(2,1)} %all-to-all-done.2.far_ref), custom_call_target="tpu_custom_call" | custom-call | tf_op jit(solution)/shard_map/pallas_call | solution.py:291
  (77 shorter events, 51.8 us)
Async XLA Ops:
  0.6 109.8 %copy-start = (bf16[512,1024]{1,0:T(8,128)(2,1)S(1)}, bf16[512,1024]{1,0:T(8,128)(2,1)}, u32[]{:S(2)}) copy-start(bf16[512,1024]{1,0:T(8,128)(2,1)} %param.8) | copy-start | bytes 3145732
  0.6 1.6 collective-permute-start
  2.2 11.9 %collective-permute-start.1 = (bf16[32,512]{1,0:T(8,128)(2,1)S(1)}, bf16[32,512]{1,0:T(8,128)(2,1)S(1)}, u32[]{:S(2)}, u32[]{:S(2)}) collective-permute-start(bf16[32,512]{1,0:T(8,128)(2,1)S(1)} %collective-permute-done), channel_id=1, source_target_pairs={{0,32},{32,64},{64,96},{96,0},{1,33},{33,65},{65,97},{97,1},{2,34}... | collective-permute-start | bytes 98312 | tf_op jit(solution)/shard_map/ppermute | solution.py:315
  6.6 7.6 %collective-permute-start.2 = (bf16[32,512]{1,0:T(8,128)(2,1)S(1)}, bf16[32,512]{1,0:T(8,128)(2,1)S(1)}, u32[]{:S(2)}, u32[]{:S(2)}) collective-permute-start(bf16[32,512]{1,0:T(8,128)(2,1)S(1)} %collective-permute-done), channel_id=1, source_target_pairs={{0,64},{32,96},{64,0},{96,32},{1,65},{33,97},{65,1},{97,33},{2,66}... | collective-permute-start | bytes 98312 | tf_op jit(solution)/shard_map/ppermute | solution.py:315
  11.5 5.0 %collective-permute-start.3 = (bf16[32,512]{1,0:T(8,128)(2,1)S(1)}, bf16[32,512]{1,0:T(8,128)(2,1)S(1)}, u32[]{:S(2)}, u32[]{:S(2)}) collective-permute-start(bf16[32,512]{1,0:T(8,128)(2,1)S(1)} %collective-permute-done), channel_id=1, source_target_pairs={{0,96},{32,0},{64,32},{96,64},{1,97},{33,1},{65,33},{97,65},{2,98}... | collective-permute-start | bytes 98312 | tf_op jit(solution)/shard_map/ppermute | solution.py:315
  16.5 43.6 %collective-permute-start.4 = (bf16[128,512]{1,0:T(8,128)(2,1)S(1)}, bf16[128,512]{1,0:T(8,128)(2,1)S(1)}, u32[]{:S(2)}, u32[]{:S(2)}) collective-permute-start(bf16[128,512]{1,0:T(8,128)(2,1)S(1)} %get-tuple-element.48), channel_id=1, source_target_pairs={{0,8},{8,16},{16,24},{24,0},{1,9},{9,17},{17,25},{25,1},{2,10},{10... | collective-permute-start | bytes 393224 | tf_op jit(solution)/shard_map/ppermute | solution.py:315
  23.8 149.4 %all-to-all-start = ((bf16[128,48,128]{2,1,0:T(8,128)(2,1)}), bf16[128,48,128]{2,1,0:T(8,128)(2,1)S(1)}, u32[]{:S(2)}, u32[]{:S(2)}) async-start(bf16[128,48,128]{2,1,0:T(8,128)(2,1)} %copy-done.1), calls=%async_computation | async-start | bytes 3145728 | tf_op jit(solution)/shard_map/all_to_all | solution.py:348
  52.5 16.5 %collective-permute-start.5 = (bf16[128,512]{1,0:T(8,128)(2,1)S(1)}, bf16[128,512]{1,0:T(8,128)(2,1)S(1)}, u32[]{:S(2)}, u32[]{:S(2)}) collective-permute-start(bf16[128,512]{1,0:T(8,128)(2,1)S(1)} %get-tuple-element.48), channel_id=1, source_target_pairs={{0,16},{8,24},{16,0},{24,8},{1,17},{9,25},{17,1},{25,9},{2,18},{10... | collective-permute-start | bytes 393224 | tf_op jit(solution)/shard_map/ppermute | solution.py:315
  57.3 16.2 %collective-permute-start.6 = (bf16[128,512]{1,0:T(8,128)(2,1)S(1)}, bf16[128,512]{1,0:T(8,128)(2,1)S(1)}, u32[]{:S(2)}, u32[]{:S(2)}) collective-permute-start(bf16[128,512]{1,0:T(8,128)(2,1)S(1)} %get-tuple-element.48), channel_id=1, source_target_pairs={{0,24},{8,0},{16,8},{24,16},{1,25},{9,1},{17,9},{25,17},{2,26},{10... | collective-permute-start | bytes 393224 | tf_op jit(solution)/shard_map/ppermute | solution.py:315
  73.6 17.8 %collective-permute-start.9 = (bf16[512,512]{1,0:T(8,128)(2,1)S(1)}, bf16[512,512]{1,0:T(8,128)(2,1)S(1)}, u32[]{:S(2)}, u32[]{:S(2)}) collective-permute-start(bf16[512,512]{1,0:T(8,128)(2,1)S(1)} %constant_dynamic-update-slice_fusion.4), channel_id=1, source_target_pairs={{0,384},{128,0},{256,128},{384,256},{1,385},{129,1},{257,129},{385... | collective-permute-start | bytes 1572872 | tf_op jit(solution)/shard_map/ppermute | solution.py:315
  77.1 18.0 %collective-permute-start.8 = (bf16[512,512]{1,0:T(8,128)(2,1)S(1)}, bf16[512,512]{1,0:T(8,128)(2,1)S(1)}, u32[]{:S(2)}, u32[]{:S(2)}) collective-permute-start(bf16[512,512]{1,0:T(8,128)(2,1)S(1)} %constant_dynamic-update-slice_fusion.4), channel_id=1, source_target_pairs={{0,256},{128,384},{256,0},{384,128},{1,257},{129,385},{257,1},{385... | collective-permute-start | bytes 1572872 | tf_op jit(solution)/shard_map/ppermute | solution.py:315
  80.5 27.2 %collective-permute-start.7 = (bf16[512,512]{1,0:T(8,128)(2,1)S(1)}, bf16[512,512]{1,0:T(8,128)(2,1)S(1)}, u32[]{:S(2)}, u32[]{:S(2)}) collective-permute-start(bf16[512,512]{1,0:T(8,128)(2,1)S(1)} %constant_dynamic-update-slice_fusion.4), channel_id=1, source_target_pairs={{0,128},{128,256},{256,384},{384,0},{1,129},{129,257},{257,385},{3... | collective-permute-start | bytes 1572872 | tf_op jit(solution)/shard_map/ppermute | solution.py:315
  108.0 6.2 %collective-permute-start.10 = (bf16[4,512,512]{2,1,0:T(8,128)(2,1)S(1)}, bf16[4,512,512]{2,1,0:T(8,128)(2,1)S(1)}, u32[]{:S(2)}, u32[]{:S(2)}) collective-permute-start(bf16[4,512,512]{2,1,0:T(8,128)(2,1)S(1)} %pad_maximum_fusion), channel_id=1, source_target_pairs={{0,4},{4,0},{1,5},{5,1},{2,6},{6,2},{3,7},{7,3},{8,12},{12,8},{9,1... | collective-permute-start | bytes 6291464 | tf_op jit(solution)/shard_map/ppermute | solution.py:349
  115.2 24.1 %collective-permute-start.12 = (bf16[256,512]{1,0:T(8,128)(2,1)S(1)}, bf16[256,512]{1,0:T(8,128)(2,1)S(1)}, u32[]{:S(2)}, u32[]{:S(2)}) collective-permute-start(bf16[256,512]{1,0:T(8,128)(2,1)S(1)} %get-tuple-element.47), channel_id=1, source_target_pairs={{0,1},{1,2},{2,3},{3,0},{4,5},{5,6},{6,7},{7,4},{8,9},{9,10},{10,1... | collective-permute-start | bytes 786440 | tf_op jit(solution)/shard_map/ppermute | solution.py:315
  123.7 44.0 %collective-permute-start.14 = (bf16[256,512]{1,0:T(8,128)(2,1)S(1)}, bf16[256,512]{1,0:T(8,128)(2,1)S(1)}, u32[]{:S(2)}, u32[]{:S(2)}) collective-permute-start(bf16[256,512]{1,0:T(8,128)(2,1)S(1)} %get-tuple-element.46), channel_id=1, source_target_pairs={{0,3},{1,0},{2,1},{3,2},{4,7},{5,4},{6,5},{7,6},{8,11},{9,8},{10,9... | collective-permute-start | bytes 786440 | tf_op jit(solution)/shard_map/ppermute | solution.py:315
  129.4 67.6 %collective-permute-start.11 = (bf16[256,512]{1,0:T(8,128)(2,1)}, bf16[256,512]{1,0:T(8,128)(2,1)S(1)}, u32[]{:S(2)}, u32[]{:S(2)}) collective-permute-start(bf16[256,512]{1,0:T(8,128)(2,1)} %slice.91), channel_id=1, source_target_pairs={{0,3},{1,0},{2,1},{3,2},{4,7},{5,4},{6,5},{7,6},{8,11},{9,8},{10,9... | collective-permute-start | bytes 786440 | tf_op jit(solution)/shard_map/ppermute | solution.py:315
  137.4 59.6 %collective-permute-start.16 = (bf16[256,512]{1,0:T(8,128)(2,1)}, bf16[256,512]{1,0:T(8,128)(2,1)S(1)}, u32[]{:S(2)}, u32[]{:S(2)}) collective-permute-start(bf16[256,512]{1,0:T(8,128)(2,1)} %slice.90), channel_id=1, source_target_pairs={{0,1},{1,2},{2,3},{3,0},{4,5},{5,6},{6,7},{7,4},{8,9},{9,10},{10,1... | collective-permute-start | bytes 786440 | tf_op jit(solution)/shard_map/ppermute | solution.py:315
  140.1 48.4 %collective-permute-start.13 = (bf16[256,512]{1,0:T(8,128)(2,1)}, bf16[256,512]{1,0:T(8,128)(2,1)S(1)}, u32[]{:S(2)}, u32[]{:S(2)}) collective-permute-start(bf16[256,512]{1,0:T(8,128)(2,1)} %fusion.51), channel_id=1, source_target_pairs={{0,1},{1,2},{2,3},{3,0},{4,5},{5,6},{6,7},{7,4},{8,9},{9,10},{10,1... | collective-permute-start | bytes 786440 | tf_op jit(solution)/shard_map/ppermute | solution.py:315
  168.4 28.6 %collective-permute-start.15 = (bf16[256,512]{1,0:T(8,128)(2,1)}, bf16[256,512]{1,0:T(8,128)(2,1)}, u32[]{:S(2)}, u32[]{:S(2)}) collective-permute-start(bf16[256,512]{1,0:T(8,128)(2,1)} %fusion.50), channel_id=1, source_target_pairs={{0,3},{1,0},{2,1},{3,2},{4,7},{5,4},{6,5},{7,6},{8,11},{9,8},{10,9... | collective-permute-start | bytes 786440 | tf_op jit(solution)/shard_map/ppermute | solution.py:315
  173.2 23.8 %copy-start.12 = (f32[512,512]{1,0:T(8,128)S(1)}, f32[512,512]{1,0:T(8,128)}, u32[]{:S(2)}) copy-start(f32[512,512]{1,0:T(8,128)} %convolution_add_fusion.2) | copy-start | bytes 3145732
  181.2 17.0 %copy-start.3 = (bf16[512,512]{1,0:T(8,128)(2,1)S(1)}, bf16[512,512]{1,0:T(8,128)(2,1)}, u32[]{:S(2)}) copy-start(bf16[512,512]{1,0:T(8,128)(2,1)} %q_ref.3) | copy-start | bytes 1572868
  181.2 17.0 %copy-start.5 = (bf16[512,512]{1,0:T(8,128)(2,1)S(1)}, bf16[512,512]{1,0:T(8,128)(2,1)}, u32[]{:S(2)}) copy-start(bf16[512,512]{1,0:T(8,128)(2,1)} %k_ref.3) | copy-start | bytes 1572868
  181.3 17.0 %copy-start.7 = (bf16[512,512]{1,0:T(8,128)(2,1)S(1)}, bf16[512,512]{1,0:T(8,128)(2,1)}, u32[]{:S(2)}) copy-start(bf16[512,512]{1,0:T(8,128)(2,1)} %v_ref.3) | copy-start | bytes 1572868
  258.2 48.0 %all-to-all-start.2 = ((bf16[128,48,128]{2,1,0:T(8,128)(2,1)}), bf16[128,48,128]{2,1,0:T(8,128)(2,1)}, u32[]{:S(2)}, u32[]{:S(2)}) async-start(bf16[128,48,128]{2,1,0:T(8,128)(2,1)} %copy-done.2), calls=%async_computation.2 | async-start | bytes 3145728 | tf_op jit(solution)/shard_map/all_to_all | solution.py:417
  (8 other events, 8.4 us)

commit v2 on v1

--- a/solution.py
+++ b/solution.py
@@ -366,8 +366,6 @@
     above, below, here = (partial(head + by, mine, others) for by in (1, -1, 0))
     far_up = shifted(opposite[low], "head", 1)
     far_down = shifted(opposite[high], "head", -1)
-    near_up = shifted(above[high].astype(BF16), "head", 1)
-    near_down = shifted(below[low].astype(BF16), "head", -1)
     last_up = shifted((far_up.astype(F32) + above[low]).astype(BF16), "head", 1)
     last_down = shifted(
         (far_down.astype(F32) + below[high]).astype(BF16), "head", -1
@@ -375,6 +373,11 @@
 
     stats = jax.ShapeDtypeStruct((32, 128), F32)
     units = pltpu.VMEM((16, 128, 128), BF16)
+    near_high, near_low, far_qkv = lax.optimization_barrier(
+        (above[high].astype(BF16), below[low].astype(BF16), far_qkv)
+    )
+    near_up = shifted(near_high, "head", 1)
+    near_down = shifted(near_low, "head", -1)
     unit_qkv, far_probs, far_out, far_columns, far_lse = call(
         far_forward_kernel,
         (far_qkv,),

time: 312 us -> 316 us (1.013)
  blocking collectives: 48.2 us -> 54.5 us
    all_to_all x1, blocking collectives: 48.2 us -> 54.5 us  [program(): crossed = lax.all_to_all(sent_grad, SEQ, 0, 0, tiled=True)]
    ppermute x15, waiting for transfers between devices: 77.7 us -> 74.4 us  [shifted(): return lax.ppermute(values, axis, [(i, (i + by) % 4) for i in range(4)])]
    unnamed x31 -> x33, local copies, waits for them, and re-layouts: 8.46 us -> 8.46 us
  transfers between devices with their start and end apart: 19 -> 19, of which waited for: 11 -> 13; matrix products, arithmetic and copies ran while one was open for 3% -> 4% of each run, Pallas kernels for 6% -> 6%
where the time goes in v2:
time: 316 us; the launch traced here: 315 us
  waiting for transfers between devices  104 us (33%)
  starting transfers between devices  102 us (32%)
  blocking collectives  54.5 us (17%)
  Pallas kernels  33.8 us (11%)
  local copies, waits for them, and re-layouts  9.28 us (3%)
  matrix products  8.42 us (3%)
    ppermute x15, waiting for transfers between devices, shifted(): return lax.ppermute(values, axis, [(i, (i + by) % 4) for i in range(4)])  74.4 us
    ppermute x15, starting transfers between devices, shifted(): return lax.ppermute(values, axis, [(i, (i + by) % 4) for i in range(4)])  62.1 us
    all_to_all x1, blocking collectives, program(): crossed = lax.all_to_all(sent_grad, SEQ, 0, 0, tiled=True)  54.5 us
    all_to_all x1, starting transfers between devices, program(): far_qkv = lax.all_to_all(sent, SEQ, 0, 0, tiled=True)  28.7 us
    all_to_all x1, waiting for transfers between devices, program(): home = lax.all_to_all(back, SEQ, 0, 0, tiled=True)  27.6 us
    pallas_call x4, Pallas kernels, call(): pl.pallas_call(kernel, out_shape=outs, in_specs=[vmem] * len(args), out_s...  25.4 us
    unnamed x33, local copies, waits for them, and re-layouts  8.46 us
    all_to_all x1, starting transfers between devices, program(): home = lax.all_to_all(back, SEQ, 0, 0, tiled=True)  7.46 us
  transfers between devices with their start and end apart: 19, of which 13 were waited for; matrix products, arithmetic and copies ran while one was open for 4% of the time, Pallas kernels for 6%

profile of v2, /device:TPU:1, one launch (start us, length us, event | category | flops | bytes accessed | tf_op | source)
XLA Modules:
  0.0 315.0 jit_solution(1689930424594248961)
XLA Ops:
  2.2 4.4 %collective-permute-start.1 = (bf16[32,512]{1,0:T(8,128)(2,1)S(1)}, bf16[32,512]{1,0:T(8,128)(2,1)S(1)}, u32[]{:S(2)}, u32[]{:S(2)}) collective-permute-start(bf16[32,512]{1,0:T(8,128)(2,1)S(1)} %collective-permute-done), channel_id=1, source_target_pairs={{0,32},{32,64},{64,96},{96,0},{1,33},{33,65},{65,97},{97,1},{2,34}... | collective-permute-start | bytes 98312 | tf_op jit(solution)/shard_map/ppermute | solution.py:315
  6.6 4.9 %collective-permute-start.2 = (bf16[32,512]{1,0:T(8,128)(2,1)S(1)}, bf16[32,512]{1,0:T(8,128)(2,1)S(1)}, u32[]{:S(2)}, u32[]{:S(2)}) collective-permute-start(bf16[32,512]{1,0:T(8,128)(2,1)S(1)} %collective-permute-done), channel_id=1, source_target_pairs={{0,64},{32,96},{64,0},{96,32},{1,65},{33,97},{65,1},{97,33},{2,66}... | collective-permute-start | bytes 98312 | tf_op jit(solution)/shard_map/ppermute | solution.py:315
  23.8 28.7 %all-to-all-start = ((bf16[128,48,128]{2,1,0:T(8,128)(2,1)}), bf16[128,48,128]{2,1,0:T(8,128)(2,1)S(1)}, u32[]{:S(2)}, u32[]{:S(2)}) async-start(bf16[128,48,128]{2,1,0:T(8,128)(2,1)} %copy-done.1), calls=%async_computation | async-start | bytes 3145728 | tf_op jit(solution)/shard_map/all_to_all | solution.py:348
  52.4 4.8 %collective-permute-start.5 = (bf16[128,512]{1,0:T(8,128)(2,1)S(1)}, bf16[128,512]{1,0:T(8,128)(2,1)S(1)}, u32[]{:S(2)}, u32[]{:S(2)}) collective-permute-start(bf16[128,512]{1,0:T(8,128)(2,1)S(1)} %get-tuple-element.54), channel_id=1, source_target_pairs={{0,16},{8,24},{16,0},{24,8},{1,17},{9,25},{17,1},{25,9},{2,18},{10... | collective-permute-start | bytes 393224 | tf_op jit(solution)/shard_map/ppermute | solution.py:315
  60.1 8.8 %collective-permute-done.5 = bf16[128,512]{1,0:T(8,128)(2,1)S(1)} collective-permute-done((bf16[128,512]{1,0:T(8,128)(2,1)S(1)}, bf16[128,512]{1,0:T(8,128)(2,1)S(1)}, u32[]{:S(2)}, u32[]{:S(2)}) %collective-permute-start.5) | collective-permute-done | bytes 131104 | tf_op jit(solution)/shard_map/ppermute | solution.py:315
  69.0 4.6 %collective-permute-done.6 = bf16[128,512]{1,0:T(8,128)(2,1)S(1)} collective-permute-done((bf16[128,512]{1,0:T(8,128)(2,1)S(1)}, bf16[128,512]{1,0:T(8,128)(2,1)S(1)}, u32[]{:S(2)}, u32[]{:S(2)}) %collective-permute-start.6) | collective-permute-done | bytes 131104 | tf_op jit(solution)/shard_map/ppermute | solution.py:315
  73.5 3.6 %collective-permute-start.9 = (bf16[512,512]{1,0:T(8,128)(2,1)S(1)}, bf16[512,512]{1,0:T(8,128)(2,1)S(1)}, u32[]{:S(2)}, u32[]{:S(2)}) collective-permute-start(bf16[512,512]{1,0:T(8,128)(2,1)S(1)} %constant_dynamic-update-slice_fusion.4), channel_id=1, source_target_pairs={{0,384},{128,0},{256,128},{384,256},{1,385},{129,1},{257,129},{385... | collective-permute-start | bytes 1572872 | tf_op jit(solution)/shard_map/ppermute | solution.py:315
  82.5 8.9 %collective-permute-done.9 = bf16[512,512]{1,0:T(8,128)(2,1)S(1)} collective-permute-done((bf16[512,512]{1,0:T(8,128)(2,1)S(1)}, bf16[512,512]{1,0:T(8,128)(2,1)S(1)}, u32[]{:S(2)}, u32[]{:S(2)}) %collective-permute-start.9) | collective-permute-done | bytes 524320 | tf_op jit(solution)/shard_map/ppermute | solution.py:315
  91.4 3.7 %collective-permute-done.8 = bf16[512,512]{1,0:T(8,128)(2,1)S(1)} collective-permute-done((bf16[512,512]{1,0:T(8,128)(2,1)S(1)}, bf16[512,512]{1,0:T(8,128)(2,1)S(1)}, u32[]{:S(2)}, u32[]{:S(2)}) %collective-permute-start.8) | collective-permute-done | bytes 524320 | tf_op jit(solution)/shard_map/ppermute | solution.py:315
  95.1 12.6 %collective-permute-done.7 = bf16[512,512]{1,0:T(8,128)(2,1)S(1)} collective-permute-done((bf16[512,512]{1,0:T(8,128)(2,1)S(1)}, bf16[512,512]{1,0:T(8,128)(2,1)S(1)}, u32[]{:S(2)}, u32[]{:S(2)}) %collective-permute-start.7) | collective-permute-done | bytes 524320 | tf_op jit(solution)/shard_map/ppermute | solution.py:315
  115.1 8.5 %collective-permute-start.12 = (bf16[256,512]{1,0:T(8,128)(2,1)S(1)}, bf16[256,512]{1,0:T(8,128)(2,1)S(1)}, u32[]{:S(2)}, u32[]{:S(2)}) collective-permute-start(bf16[256,512]{1,0:T(8,128)(2,1)S(1)} %get-tuple-element.53), channel_id=1, source_target_pairs={{0,1},{1,2},{2,3},{3,0},{4,5},{5,6},{6,7},{7,4},{8,9},{9,10},{10,1... | collective-permute-start | bytes 786440 | tf_op jit(solution)/shard_map/ppermute | solution.py:315
  130.4 6.6 %collective-permute-done.12 = bf16[256,512]{1,0:T(8,128)(2,1)S(1)} collective-permute-done((bf16[256,512]{1,0:T(8,128)(2,1)S(1)}, bf16[256,512]{1,0:T(8,128)(2,1)S(1)}, u32[]{:S(2)}, u32[]{:S(2)}) %collective-permute-start.12) | collective-permute-done | bytes 262176 | tf_op jit(solution)/shard_map/ppermute | solution.py:315
  137.7 7.3 %collective-permute-start.13 = (bf16[256,512]{1,0:T(8,128)(2,1)}, bf16[256,512]{1,0:T(8,128)(2,1)S(1)}, u32[]{:S(2)}, u32[]{:S(2)}) collective-permute-start(bf16[256,512]{1,0:T(8,128)(2,1)} %fusion.51), channel_id=1, source_target_pairs={{0,1},{1,2},{2,3},{3,0},{4,5},{5,6},{6,7},{7,4},{8,9},{9,10},{10,1... | collective-permute-start | bytes 786440 | tf_op jit(solution)/shard_map/ppermute | solution.py:315
  145.1 4.2 %collective-permute-done.14 = bf16[256,512]{1,0:T(8,128)(2,1)S(1)} collective-permute-done((bf16[256,512]{1,0:T(8,128)(2,1)S(1)}, bf16[256,512]{1,0:T(8,128)(2,1)S(1)}, u32[]{:S(2)}, u32[]{:S(2)}) %collective-permute-start.14) | collective-permute-done | bytes 262176 | tf_op jit(solution)/shard_map/ppermute | solution.py:315
  153.4 7.1 %collective-permute-start.11 = (bf16[256,512]{1,0:T(8,128)(2,1)}, bf16[256,512]{1,0:T(8,128)(2,1)S(1)}, u32[]{:S(2)}, u32[]{:S(2)}) collective-permute-start(bf16[256,512]{1,0:T(8,128)(2,1)} %slice.90), channel_id=1, source_target_pairs={{0,3},{1,0},{2,1},{3,2},{4,7},{5,4},{6,5},{7,6},{8,11},{9,8},{10,9... | collective-permute-start | bytes 786440 | tf_op jit(solution)/shard_map/ppermute | solution.py:315
  164.7 8.0 %shard_map.85 = (bf16[3,16,128,128]{3,2,1,0:T(8,128)(2,1)S(1)}, f32[16,128,128]{2,1,0:T(8,128)S(1)}, bf16[128,16,128]{2,1,0:T(8,128)(2,1)S(1)}, bf16[128,128]{1,0:T(8,128)(2,1)S(1)}, f32[32,128]{1,0:T(8,128)S(1)}) custom-call(bf16[128,48,128]{2,1,0:T(8,128)(2,1)S(1)} %all-to-all-done.qkv_ref), custom_call_target="tpu_custom_call" | custom-call | tf_op jit(solution)/shard_map/pallas_call | solution.py:304
  175.4 7.3 %collective-permute-done.11 = bf16[256,512]{1,0:T(8,128)(2,1)S(1)} collective-permute-done((bf16[256,512]{1,0:T(8,128)(2,1)}, bf16[256,512]{1,0:T(8,128)(2,1)S(1)}, u32[]{:S(2)}, u32[]{:S(2)}) %collective-permute-start.11) | collective-permute-done | bytes 262176 | tf_op jit(solution)/shard_map/ppermute | solution.py:315
  182.8 12.6 %collective-permute-done.16 = bf16[256,512]{1,0:T(8,128)(2,1)S(1)} collective-permute-done((bf16[256,512]{1,0:T(8,128)(2,1)S(1)}, bf16[256,512]{1,0:T(8,128)(2,1)S(1)}, u32[]{:S(2)}, u32[]{:S(2)}) %collective-permute-start.16) | collective-permute-done | bytes 262176 | tf_op jit(solution)/shard_map/ppermute | solution.py:315
  198.4 54.5 %all_to_all.15.far_ref.g_ref = bf16[128,40,128]{2,1,0:T(8,128)(2,1)S(1)} all-to-all(bf16[128,40,128]{2,1,0:T(8,128)(2,1)S(1)} %get-tuple-element.39), channel_id=1, replica_groups=mesh['x'=4,'zl'=4,'y'=4,'core'=2,'head'=4] {'x','zl','y','core'}, dimensions={0} | all-to-all | bytes 2621440 | tf_op jit(solution)/shard_map/all_to_all | solution.py:413
  252.9 7.8 %shard_map.88 = bf16[128,48,128]{2,1,0:T(8,128)(2,1)S(1)} custom-call(bf16[3,16,128,128]{3,2,1,0:T(8,128)(2,1)S(1)} %get-tuple-element.44.unit_ref, f32[16,128,128]{2,1,0:T(8,128)S(1)} %get-tuple-element.45.probs_ref, f32[32,128]{1,0:T(8,128)S(1)} %get-tuple-element.46.lse_ref, bf16[128,40,128]{2,1,0:T(8,128)(2,1)S(1)} %all_to_all.15.far_ref.g_ref), custom_call_target="tpu_custom_call" | custom-call | tf_op jit(solution)/shard_map/pallas_call | solution.py:304
  261.9 7.5 %all-to-all-start.2 = ((bf16[128,48,128]{2,1,0:T(8,128)(2,1)}), bf16[128,48,128]{2,1,0:T(8,128)(2,1)}, u32[]{:S(2)}, u32[]{:S(2)}) async-start(bf16[128,48,128]{2,1,0:T(8,128)(2,1)} %copy-done.2), calls=%async_computation.2 | async-start | bytes 3145728 | tf_op jit(solution)/shard_map/all_to_all | solution.py:420
  272.5 6.8 %shard_map.87 = (bf16[512,512]{1,0:T(8,128)(2,1)}, f32[512,512]{1,0:T(8,128)S(1)}, f32[512,512]{1,0:T(8,128)S(1)}, f32[512,512]{1,0:T(8,128)S(1)}) custom-call(bf16[512,512]{1,0:T(8,128)(2,1)S(1)} %copy-done.4, bf16[512,512]{1,0:T(8,128)(2,1)S(1)} %copy-done.6, bf16[512,512]{1,0:T(8,128)(2,1)S(1)} %copy-done.8, ...), custom_call_target="tpu_custom_call" | custom-call | tf_op jit(solution)/shard_map/pallas_call | solution.py:304
  282.2 27.6 %all-to-all-done.2.far_ref = bf16[128,48,128]{2,1,0:T(8,128)(2,1)} async-done(((bf16[128,48,128]{2,1,0:T(8,128)(2,1)}), bf16[128,48,128]{2,1,0:T(8,128)(2,1)}, u32[]{:S(2)}, u32[]{:S(2)}) %all-to-all-start.2) | async-done | bytes 1572896 | tf_op jit(solution)/shard_map/all_to_all | solution.py:420
  309.8 5.2 %shard_map.89 = (bf16[512,512]{1,0:T(8,128)(2,1)}, bf16[512,512]{1,0:T(8,128)(2,1)}, bf16[512,512]{1,0:T(8,128)(2,1)}) custom-call(f32[512,512]{1,0:T(8,128)} %copy-done.9, f32[512,512]{1,0:T(8,128)} %copy-done.10, f32[512,512]{1,0:T(8,128)} %copy-done.11, bf16[128,48,128]{2,1,0:T(8,128)(2,1)} %all-to-all-done.2.far_ref), custom_call_target="tpu_custom_call" | custom-call | tf_op jit(solution)/shard_map/pallas_call | solution.py:291
  (79 shorter events, 58.0 us)
Async XLA Ops:
  0.6 109.8 %copy-start = (bf16[512,1024]{1,0:T(8,128)(2,1)S(1)}, bf16[512,1024]{1,0:T(8,128)(2,1)}, u32[]{:S(2)}) copy-start(bf16[512,1024]{1,0:T(8,128)(2,1)} %param.8) | copy-start | bytes 3145732
  0.6 1.6 collective-permute-start
  2.2 11.9 %collective-permute-start.1 = (bf16[32,512]{1,0:T(8,128)(2,1)S(1)}, bf16[32,512]{1,0:T(8,128)(2,1)S(1)}, u32[]{:S(2)}, u32[]{:S(2)}) collective-permute-start(bf16[32,512]{1,0:T(8,128)(2,1)S(1)} %collective-permute-done), channel_id=1, source_target_pairs={{0,32},{32,64},{64,96},{96,0},{1,33},{33,65},{65,97},{97,1},{2,34}... | collective-permute-start | bytes 98312 | tf_op jit(solution)/shard_map/ppermute | solution.py:315
  6.6 7.6 %collective-permute-start.2 = (bf16[32,512]{1,0:T(8,128)(2,1)S(1)}, bf16[32,512]{1,0:T(8,128)(2,1)S(1)}, u32[]{:S(2)}, u32[]{:S(2)}) collective-permute-start(bf16[32,512]{1,0:T(8,128)(2,1)S(1)} %collective-permute-done), channel_id=1, source_target_pairs={{0,64},{32,96},{64,0},{96,32},{1,65},{33,97},{65,1},{97,33},{2,66}... | collective-permute-start | bytes 98312 | tf_op jit(solution)/shard_map/ppermute | solution.py:315
  11.5 5.0 %collective-permute-start.3 = (bf16[32,512]{1,0:T(8,128)(2,1)S(1)}, bf16[32,512]{1,0:T(8,128)(2,1)S(1)}, u32[]{:S(2)}, u32[]{:S(2)}) collective-permute-start(bf16[32,512]{1,0:T(8,128)(2,1)S(1)} %collective-permute-done), channel_id=1, source_target_pairs={{0,96},{32,0},{64,32},{96,64},{1,97},{33,1},{65,33},{97,65},{2,98}... | collective-permute-start | bytes 98312 | tf_op jit(solution)/shard_map/ppermute | solution.py:315
  16.5 43.6 %collective-permute-start.4 = (bf16[128,512]{1,0:T(8,128)(2,1)S(1)}, bf16[128,512]{1,0:T(8,128)(2,1)S(1)}, u32[]{:S(2)}, u32[]{:S(2)}) collective-permute-start(bf16[128,512]{1,0:T(8,128)(2,1)S(1)} %get-tuple-element.54), channel_id=1, source_target_pairs={{0,8},{8,16},{16,24},{24,0},{1,9},{9,17},{17,25},{25,1},{2,10},{10... | collective-permute-start | bytes 393224 | tf_op jit(solution)/shard_map/ppermute | solution.py:315
  23.8 129.7 %all-to-all-start = ((bf16[128,48,128]{2,1,0:T(8,128)(2,1)}), bf16[128,48,128]{2,1,0:T(8,128)(2,1)S(1)}, u32[]{:S(2)}, u32[]{:S(2)}) async-start(bf16[128,48,128]{2,1,0:T(8,128)(2,1)} %copy-done.1), calls=%async_computation | async-start | bytes 3145728 | tf_op jit(solution)/shard_map/all_to_all | solution.py:348
  52.4 16.5 %collective-permute-start.5 = (bf16[128,512]{1,0:T(8,128)(2,1)S(1)}, bf16[128,512]{1,0:T(8,128)(2,1)S(1)}, u32[]{:S(2)}, u32[]{:S(2)}) collective-permute-start(bf16[128,512]{1,0:T(8,128)(2,1)S(1)} %get-tuple-element.54), channel_id=1, source_target_pairs={{0,16},{8,24},{16,0},{24,8},{1,17},{9,25},{17,1},{25,9},{2,18},{10... | collective-permute-start | bytes 393224 | tf_op jit(solution)/shard_map/ppermute | solution.py:315
  57.3 16.2 %collective-permute-start.6 = (bf16[128,512]{1,0:T(8,128)(2,1)S(1)}, bf16[128,512]{1,0:T(8,128)(2,1)S(1)}, u32[]{:S(2)}, u32[]{:S(2)}) collective-permute-start(bf16[128,512]{1,0:T(8,128)(2,1)S(1)} %get-tuple-element.54), channel_id=1, source_target_pairs={{0,24},{8,0},{16,8},{24,16},{1,25},{9,1},{17,9},{25,17},{2,26},{10... | collective-permute-start | bytes 393224 | tf_op jit(solution)/shard_map/ppermute | solution.py:315
  73.5 17.8 %collective-permute-start.9 = (bf16[512,512]{1,0:T(8,128)(2,1)S(1)}, bf16[512,512]{1,0:T(8,128)(2,1)S(1)}, u32[]{:S(2)}, u32[]{:S(2)}) collective-permute-start(bf16[512,512]{1,0:T(8,128)(2,1)S(1)} %constant_dynamic-update-slice_fusion.4), channel_id=1, source_target_pairs={{0,384},{128,0},{256,128},{384,256},{1,385},{129,1},{257,129},{385... | collective-permute-start | bytes 1572872 | tf_op jit(solution)/shard_map/ppermute | solution.py:315
  77.1 18.0 %collective-permute-start.8 = (bf16[512,512]{1,0:T(8,128)(2,1)S(1)}, bf16[512,512]{1,0:T(8,128)(2,1)S(1)}, u32[]{:S(2)}, u32[]{:S(2)}) collective-permute-start(bf16[512,512]{1,0:T(8,128)(2,1)S(1)} %constant_dynamic-update-slice_fusion.4), channel_id=1, source_target_pairs={{0,256},{128,384},{256,0},{384,128},{1,257},{129,385},{257,1},{385... | collective-permute-start | bytes 1572872 | tf_op jit(solution)/shard_map/ppermute | solution.py:315
  80.5 27.2 %collective-permute-start.7 = (bf16[512,512]{1,0:T(8,128)(2,1)S(1)}, bf16[512,512]{1,0:T(8,128)(2,1)S(1)}, u32[]{:S(2)}, u32[]{:S(2)}) collective-permute-start(bf16[512,512]{1,0:T(8,128)(2,1)S(1)} %constant_dynamic-update-slice_fusion.4), channel_id=1, source_target_pairs={{0,128},{128,256},{256,384},{384,0},{1,129},{129,257},{257,385},{3... | collective-permute-start | bytes 1572872 | tf_op jit(solution)/shard_map/ppermute | solution.py:315
  108.0 6.2 %collective-permute-start.10 = (bf16[4,512,512]{2,1,0:T(8,128)(2,1)S(1)}, bf16[4,512,512]{2,1,0:T(8,128)(2,1)S(1)}, u32[]{:S(2)}, u32[]{:S(2)}) collective-permute-start(bf16[4,512,512]{2,1,0:T(8,128)(2,1)S(1)} %pad_maximum_fusion), channel_id=1, source_target_pairs={{0,4},{4,0},{1,5},{5,1},{2,6},{6,2},{3,7},{7,3},{8,12},{12,8},{9,1... | collective-permute-start | bytes 6291464 | tf_op jit(solution)/shard_map/ppermute | solution.py:349
  112.6 15.6 %copy-start.12 = (bf16[512,1024]{0,1:T(8,128)(2,1)}, bf16[512,1024]{0,1:T(8,128)(2,1)S(1)}, u32[]{:S(2)}) copy-start(bf16[512,1024]{0,1:T(8,128)(2,1)S(1)} %fusion.45) | copy-start | bytes 3145732
  115.1 21.8 %collective-permute-start.12 = (bf16[256,512]{1,0:T(8,128)(2,1)S(1)}, bf16[256,512]{1,0:T(8,128)(2,1)S(1)}, u32[]{:S(2)}, u32[]{:S(2)}) collective-permute-start(bf16[256,512]{1,0:T(8,128)(2,1)S(1)} %get-tuple-element.53), channel_id=1, source_target_pairs={{0,1},{1,2},{2,3},{3,0},{4,5},{5,6},{6,7},{7,4},{8,9},{9,10},{10,1... | collective-permute-start | bytes 786440 | tf_op jit(solution)/shard_map/ppermute | solution.py:315
  123.6 25.6 %collective-permute-start.14 = (bf16[256,512]{1,0:T(8,128)(2,1)S(1)}, bf16[256,512]{1,0:T(8,128)(2,1)S(1)}, u32[]{:S(2)}, u32[]{:S(2)}) collective-permute-start(bf16[256,512]{1,0:T(8,128)(2,1)S(1)} %get-tuple-element.52), channel_id=1, source_target_pairs={{0,3},{1,0},{2,1},{3,2},{4,7},{5,4},{6,5},{7,6},{8,11},{9,8},{10,9... | collective-permute-start | bytes 786440 | tf_op jit(solution)/shard_map/ppermute | solution.py:315
  137.7 35.0 %collective-permute-start.13 = (bf16[256,512]{1,0:T(8,128)(2,1)}, bf16[256,512]{1,0:T(8,128)(2,1)S(1)}, u32[]{:S(2)}, u32[]{:S(2)}) collective-permute-start(bf16[256,512]{1,0:T(8,128)(2,1)} %fusion.51), channel_id=1, source_target_pairs={{0,1},{1,2},{2,3},{3,0},{4,5},{5,6},{6,7},{7,4},{8,9},{9,10},{10,1... | collective-permute-start | bytes 786440 | tf_op jit(solution)/shard_map/ppermute | solution.py:315
  150.0 25.4 %collective-permute-start.15 = (bf16[256,512]{1,0:T(8,128)(2,1)}, bf16[256,512]{1,0:T(8,128)(2,1)S(1)}, u32[]{:S(2)}, u32[]{:S(2)}) collective-permute-start(bf16[256,512]{1,0:T(8,128)(2,1)} %fusion.50), channel_id=1, source_target_pairs={{0,3},{1,0},{2,1},{3,2},{4,7},{5,4},{6,5},{7,6},{8,11},{9,8},{10,9... | collective-permute-start | bytes 786440 | tf_op jit(solution)/shard_map/ppermute | solution.py:315
  153.4 29.3 %collective-permute-start.11 = (bf16[256,512]{1,0:T(8,128)(2,1)}, bf16[256,512]{1,0:T(8,128)(2,1)S(1)}, u32[]{:S(2)}, u32[]{:S(2)}) collective-permute-start(bf16[256,512]{1,0:T(8,128)(2,1)} %slice.90), channel_id=1, source_target_pairs={{0,3},{1,0},{2,1},{3,2},{4,7},{5,4},{6,5},{7,6},{8,11},{9,8},{10,9... | collective-permute-start | bytes 786440 | tf_op jit(solution)/shard_map/ppermute | solution.py:315
  160.5 34.8 %collective-permute-start.16 = (bf16[256,512]{1,0:T(8,128)(2,1)S(1)}, bf16[256,512]{1,0:T(8,128)(2,1)S(1)}, u32[]{:S(2)}, u32[]{:S(2)}) collective-permute-start(bf16[256,512]{1,0:T(8,128)(2,1)S(1)} %slice.91), channel_id=1, source_target_pairs={{0,1},{1,2},{2,3},{3,0},{4,5},{5,6},{6,7},{7,4},{8,9},{9,10},{10,1... | collective-permute-start | bytes 786440 | tf_op jit(solution)/shard_map/ppermute | solution.py:315
  172.7 22.9 %copy-start.3 = (bf16[512,512]{1,0:T(8,128)(2,1)S(1)}, bf16[512,512]{1,0:T(8,128)(2,1)}, u32[]{:S(2)}) copy-start(bf16[512,512]{1,0:T(8,128)(2,1)} %q_ref.3) | copy-start | bytes 1572868
  172.7 22.9 %copy-start.5 = (bf16[512,512]{1,0:T(8,128)(2,1)S(1)}, bf16[512,512]{1,0:T(8,128)(2,1)}, u32[]{:S(2)}) copy-start(bf16[512,512]{1,0:T(8,128)(2,1)} %k_ref.3) | copy-start | bytes 1572868
  172.7 22.9 %copy-start.7 = (bf16[512,512]{1,0:T(8,128)(2,1)S(1)}, bf16[512,512]{1,0:T(8,128)(2,1)}, u32[]{:S(2)}) copy-start(bf16[512,512]{1,0:T(8,128)(2,1)} %v_ref.3) | copy-start | bytes 1572868
  261.9 48.0 %all-to-all-start.2 = ((bf16[128,48,128]{2,1,0:T(8,128)(2,1)}), bf16[128,48,128]{2,1,0:T(8,128)(2,1)}, u32[]{:S(2)}, u32[]{:S(2)}) async-start(bf16[128,48,128]{2,1,0:T(8,128)(2,1)} %copy-done.2), calls=%async_computation.2 | async-start | bytes 3145728 | tf_op jit(solution)/shard_map/all_to_all | solution.py:420
  (9 other events, 21.9 us)
